TPU v7x, 128 devices: a whole 4x4x4 slice. The times are simulated.
128 devices in a mesh: wall: 8 (over y, core), cell: 16 (over x, z).
Axes of the slice: x: 4, y: 4, z: 4, core: 2. Of those that a mesh axis runs over, the one named last changes fastest.
Arguments:
- cell_points: float32 [256, 3, 544], P(('wall', 'cell')), may hold values from -4 to 64, as said below
- cell_force: float32 [256, 3, 544], P(('wall', 'cell')), may hold values from -120 to 120
- cell_weight: float32 [256, 544], P(('wall', 'cell')), may hold values from 0.01 to 0.05
- partners: int32 [256, 8], P(('wall', 'cell')), may hold values from -1 to 31, as said below
- wall_points: float32 [3, 98304], P(None, ('wall', 'cell')), may hold values from -4 to 64, as said below
- wall_area: float32 [98304], P(('wall', 'cell')), may hold values from 0.01 to 0.04
- wall_data: float32 [3, 98304], P(None, ('wall', 'cell')), may hold values from -30 to 30
Outputs:
- cell_velocity: float32 [256, 3, 544], P(('wall', 'cell'))
- wall_density: float32 [3, 98304], P(None, ('wall', 'cell'))
Inputs may be any that keep to these rules, and one draw needn't show every extreme that they name: `partners`: cell numbers within the segment or -1. Cell n of a segment is held by device n // 2 of that segment. No cell names itself. Among the rows of one device, at most 2 entries name cells of any one device, and some device is named exactly 2 times there. `cell_points`: points of closed surfaces of radius about one inside the vessel of segment s, which runs from 8 s to 8 s + 8 along the first coordinate. `wall_points`: points on the vessel wall of radius 4 about the first coordinate axis; the points of segment s lie between 8 s and 8 s + 8 along it.
All inputs are finite; a program needn't handle non-finite values.
Results may differ from a plain program's by a relative error of at most 0.0003.
Values sent between devices are 32-bit elements; how exact they have to be, the bound alone decides.
No kernel may reach another device: no remote copies, remote signals or barrier semaphores. Data moves between devices by JAX's collectives and lax.ppermute only.
A program may use at most 64 MiB of HBM per device.

v0:
```python
import math

import jax
import jax.numpy as jnp
from jax import lax
from jax.sharding import Mesh
from jax.sharding import PartitionSpec as P

ITERS = 4
WALL_CELL = ("wall_0", "wall_1", "cell_0", "cell_1")
CELL = ("cell_0", "cell_1")


blob_width = 0.1
norm_floor = 1e-06


def one_axis_at_a_time(x, axes):
    for axis in axes:
        x = lax.psum(x, axis)
    return x


def from_everyone(x, axis):
    length = lax.axis_size(axis)
    return lax.all_to_all(jnp.broadcast_to(x[None], (length, *x.shape)), axis, 0, 0, tiled=True)


def in_order(tiles, dim):
    tiles = jnp.moveaxis(tiles, 0, dim)
    dims = tiles.shape
    return tiles.reshape(*dims[:dim], dims[dim] * dims[dim + 1], *dims[dim + 2 :])


def gathered_copies(x, axis, dim):
    tiles = from_everyone(x, axis)
    return in_order(tiles, dim)


def sent_together(arrays, axis, dim, along):
    both = jnp.concatenate(arrays, axis=along)
    out, at, outs = (gathered_copies(both, axis, dim), 0, [])
    for a in arrays:
        outs.append(lax.slice_in_dim(out, at, at + a.shape[along], axis=along))
        at += a.shape[along]
    return tuple(outs)


def sent_together_2(arrays, axis, dim, along):
    widths = [a.shape[along] for a in arrays]
    both = jnp.concatenate(arrays, axis=along)
    out = lax.all_gather(both, axis, axis=dim, tiled=True)
    return tuple(jnp.split(out, [sum(widths[:k]) for k in range(1, len(widths))], axis=along))


def stokeslet(targets, sources, strength):
    offsets = targets[:, :, None] - sources[:, None, :]
    square_dist = jnp.sum(offsets * offsets, axis=0)
    shifted = square_dist + blob_width * blob_width
    factor = 1.0 / (8.0 * math.pi * shifted * jnp.sqrt(shifted))
    projected = jnp.sum(strength[:, None, :] * offsets, axis=0)
    terms = (square_dist + 2.0 * blob_width * blob_width)[None] * strength[:, None, :] + projected[
        None
    ] * offsets
    return jnp.sum(factor[None] * terms, axis=2)


def field_blocks(targets, sources, strength, block):
    count = sources.shape[1] // block
    source_blocks = jnp.transpose(sources.reshape(3, count, block), (1, 0, 2))
    strength_blocks = jnp.transpose(strength.reshape(3, count, block), (1, 0, 2))

    def add_block(carry, pieces):
        return (carry + stokeslet(targets, pieces[0], pieces[1]), None)

    total, unused = lax.scan(
        add_block, jnp.zeros(targets.shape, jnp.float32), (source_blocks, strength_blocks)
    )
    return total


def near_cell(own_points, own_strength, more_points, more_strength):
    all_points = jnp.concatenate([own_points[None], more_points], axis=0)
    all_strength = jnp.concatenate([own_strength[None], more_strength], axis=0)

    def add_source(carry, pieces):
        return (carry + stokeslet(own_points, pieces[0], pieces[1]), None)

    total, unused = lax.scan(
        add_source, jnp.zeros(own_points.shape, jnp.float32), (all_points, all_strength)
    )
    return total


def solve_small(hess, beta):
    size = len(hess[0])
    upper = [[hess[row][column] for column in range(size)] for row in range(size + 1)]
    targets = [beta] + [jnp.zeros((), jnp.float32) for column in range(size)]
    cosines = []
    sines = []
    for column in range(size):
        for prior in range(column):
            first_val = upper[prior][column]
            second_val = upper[prior + 1][column]
            upper[prior][column] = cosines[prior] * first_val + sines[prior] * second_val
            upper[prior + 1][column] = -sines[prior] * first_val + cosines[prior] * second_val
        first_val = upper[column][column]
        second_val = upper[column + 1][column]
        radius = jnp.sqrt(first_val * first_val + second_val * second_val)
        cosines.append(first_val / radius)
        sines.append(second_val / radius)
        upper[column][column] = radius
        targets[column + 1] = -sines[column] * targets[column]
        targets[column] = cosines[column] * targets[column]
    weights = [None for column in range(size)]
    for column in reversed(range(size)):
        partial_val = targets[column]
        for later in range(column + 1, size):
            partial_val = partial_val - upper[column][later] * weights[later]
        weights[column] = partial_val / upper[column][column]
    return weights


def global_norm(vector):
    return jnp.sqrt(one_axis_at_a_time(jnp.sum(vector * vector), WALL_CELL) + norm_floor)


def per_device(cell_points, cell_force, cell_weight, partners, wall_points, wall_area, wall_data):
    cell_count = cell_points.shape[0]
    slot_count = partners.shape[1]
    surface = cell_points.shape[2]
    strength = cell_force * cell_weight[:, None, :]
    packed = jnp.concatenate([cell_points, strength], axis=1)
    wanted = partners.reshape(-1)
    everyone = gathered_copies(packed, CELL, 0)
    total_cells = everyone.shape[0]
    selection = (wanted[:, None] == jnp.arange(total_cells, dtype=jnp.int32)[None, :]).astype(
        jnp.float32
    )
    picked_rows = jnp.dot(
        selection, everyone.reshape(total_cells, 6 * surface), precision=lax.Precision.HIGHEST
    )
    partner_data = picked_rows.reshape(cell_count, slot_count, 6, surface)
    near = lax.map(
        lambda pieces: near_cell(pieces[0], pieces[1], pieces[2][:, :3], pieces[2][:, 3:]),
        (cell_points, strength, partner_data),
    )
    block = wall_points.shape[1]
    beta = global_norm(wall_data)
    basis = [wall_data / beta]
    zero_val = jnp.zeros((), jnp.float32)
    hess = [[zero_val for column in range(ITERS)] for row in range(ITERS + 1)]
    for column in range(ITERS):
        vector = basis[column]
        source_strength = vector * wall_area[None, :]
        add_pieces = sent_together((wall_points, source_strength), CELL, 1, 0)
        field = field_blocks(wall_points, add_pieces[0], add_pieces[1], block)
        work = 0.5 * vector + field
        local_terms = jnp.stack([jnp.sum(work * basis[row]) for row in range(column + 1)])
        coeffs = one_axis_at_a_time(local_terms, WALL_CELL)
        for row in range(column + 1):
            hess[row][column] = coeffs[row]
            work = work - coeffs[row] * basis[row]
        scale_val = global_norm(work)
        hess[column + 1][column] = scale_val
        basis.append(work / scale_val)
    weights = solve_small(hess, beta)
    density = weights[0] * basis[0]
    for column in range(1, ITERS):
        density = density + weights[column] * basis[column]
    density_strength = density * wall_area[None, :]
    pieces = sent_together_2((wall_points, density_strength), CELL, 1, 0)
    sources = pieces[0]
    strengths = pieces[1]
    wall_part = lax.map(lambda target: field_blocks(target, sources, strengths, block), cell_points)
    return (near + wall_part, density)


def solution(mesh):
    torus = Mesh(mesh.devices.reshape(4, 2, 4, 4), ("wall_0", "wall_1", "cell_0", "cell_1"))
    in_specs = (
        P(WALL_CELL, None, None),
        P(WALL_CELL, None, None),
        P(WALL_CELL, None),
        P(WALL_CELL, None),
        P(None, WALL_CELL),
        P(WALL_CELL),
        P(None, WALL_CELL),
    )
    out_specs = (P(WALL_CELL, None, None), P(None, WALL_CELL))
    return jax.shard_map(
        per_device, mesh=torus, in_specs=in_specs, out_specs=out_specs, check_vma=False
    )
```

profile of v0, /device:TPU:1, one launch (start us, length us, event | category | flops | bytes accessed | tf_op | source)
XLA Modules:
  0.0 893.8 jit_solution(16424658115499800118)
XLA Ops:
  1.9 10.1 %psum.252 = f32[]{:T(128)} all-reduce(f32[]{:T(128)} %multiply_reduce_fusion.14), channel_id=1, replica_groups=mesh['wall_0'=4,'wall_1'=2,'cell_0'=4,'cell_1'=4] {'wall_0'}, use_global_device_ids=true, to_apply=%region_8.9 | all-reduce | flops 1 | bytes 8 | tf_op jit(solution)/shard_map/psum | solution.py:20
  12.1 5.4 psum.253
  17.5 9.1 %psum.254 = f32[]{:T(128)} all-reduce(f32[]{:T(128)} %psum.253), channel_id=1, replica_groups=mesh['wall_0'=4,'wall_1'=2,'cell_0'=4,'cell_1'=4] {'cell_0'}, use_global_device_ids=true, to_apply=%region_10.11 | all-reduce | flops 1 | bytes 8 | tf_op jit(solution)/shard_map/psum | solution.py:20
  26.6 10.4 %psum.255 = f32[]{:T(128)} all-reduce(f32[]{:T(128)} %psum.254), channel_id=1, replica_groups=mesh['wall_0'=4,'wall_1'=2,'cell_0'=4,'cell_1'=4] {'cell_1'}, use_global_device_ids=true, to_apply=%region_11.12 | all-reduce | flops 1 | bytes 8 | tf_op jit(solution)/shard_map/psum | solution.py:20
  39.9 3.6 all-to-all-start.1
  43.4 7.9 all-to-all-done.1
  51.5 94.3 %while.90 = (s32[]{:T(128)}, f32[3,768]{1,0:T(4,128)S(1)}, f32[3,768]{1,0:T(4,128)}, f32[16,3,768]{2,1,0:T(4,128)S(1)}, f32[16,3,768]{2,1,0:T(4,128)S(1)}, /*index=5*/s32[]{:T(128)}, s32[]{:T(128)}) while((s32[]{:T(128)}, f32[3,768]{1,0:T(4,128)S(1)}, f32[3,768]{1,0:T(4,128)}, f32[16,3,768]{2,1,0:T(4,128)S(1)}, ...), condition=%wide.region_16.17_spmd.clone, body=%wide.region_12.16_spmd.clone.sunk | while | flops 21235968 | bytes 19040372 | solution.py:76
  51.5 2.5 fusion.55
  57.4 2.5 fusion.55
  63.3 2.5 fusion.55
  69.2 2.5 fusion.55
  75.1 2.5 fusion.55
  81.0 2.5 fusion.55
  146.4 6.6 psum.256
  153.0 10.0 %psum.257 = f32[1]{0:T(128)} all-reduce(f32[1]{0:T(128)} %psum.256), channel_id=1, replica_groups=mesh['wall_0'=4,'wall_1'=2,'cell_0'=4,'cell_1'=4] {'wall_1'}, use_global_device_ids=true, to_apply=%region_19.20 | all-reduce | flops 1 | bytes 8 | tf_op jit(solution)/shard_map/psum | solution.py:20
  163.0 7.6 psum.258
  170.6 7.0 psum.259
  178.9 8.3 psum.260
  187.2 9.1 %psum.261 = f32[]{:T(128)} all-reduce(f32[]{:T(128)} %psum.260), channel_id=1, replica_groups=mesh['wall_0'=4,'wall_1'=2,'cell_0'=4,'cell_1'=4] {'wall_1'}, use_global_device_ids=true, to_apply=%region_24.25 | all-reduce | flops 1 | bytes 8 | tf_op jit(solution)/shard_map/psum | solution.py:20
  196.3 7.4 psum.262
  203.7 7.3 psum.263
  213.9 3.6 all-to-all-start.2
  217.5 7.9 all-to-all-done.2
  225.5 94.3 %while.91 = (s32[]{:T(128)}, f32[3,768]{1,0:T(4,128)S(1)}, f32[3,768]{1,0:T(4,128)}, f32[16,3,768]{2,1,0:T(4,128)S(1)}, f32[16,3,768]{2,1,0:T(4,128)S(1)}, /*index=5*/s32[]{:T(128)}, s32[]{:T(128)}) while((s32[]{:T(128)}, f32[3,768]{1,0:T(4,128)S(1)}, f32[3,768]{1,0:T(4,128)}, f32[16,3,768]{2,1,0:T(4,128)S(1)}, ...), condition=%wide.region_31.32_spmd.clone, body=%wide.region_27.31_spmd.clone.sunk | while | flops 21235968 | bytes 19040372 | solution.py:76
  321.8 6.0 psum.264
  327.7 9.4 %psum.265 = f32[2]{0:T(128)S(1)} all-reduce(f32[2]{0:T(128)S(1)} %psum.264), channel_id=1, replica_groups=mesh['wall_0'=4,'wall_1'=2,'cell_0'=4,'cell_1'=4] {'wall_1'}, use_global_device_ids=true, to_apply=%region_35.36 | all-reduce | flops 2 | bytes 16 | tf_op jit(solution)/shard_map/psum | solution.py:20
  337.1 7.0 psum.266
  344.1 6.3 psum.267
  353.0 8.3 psum.268
  361.3 9.1 %psum.269 = f32[]{:T(128)} all-reduce(f32[]{:T(128)} %psum.268), channel_id=1, replica_groups=mesh['wall_0'=4,'wall_1'=2,'cell_0'=4,'cell_1'=4] {'wall_1'}, use_global_device_ids=true, to_apply=%region_40.41 | all-reduce | flops 1 | bytes 8 | tf_op jit(solution)/shard_map/psum | solution.py:20
  370.5 7.4 psum.270
  377.9 7.2 psum.271
  387.3 3.6 all-to-all-start.3
  392.9 5.9 all-to-all-done.3
  399.7 3.7 all-to-all-start
  403.6 82.6 %while.92 = (s32[]{:T(128)}, f32[3,768]{1,0:T(4,128)S(1)}, f32[3,768]{1,0:T(4,128)S(1)}, f32[16,3,768]{2,1,0:T(4,128)S(1)}, f32[16,3,768]{2,1,0:T(4,128)S(1)}, /*index=5*/s32[]{:T(128)}, s32[]{:T(128)}) while((s32[]{:T(128)}, f32[3,768]{1,0:T(4,128)S(1)}, f32[3,768]{1,0:T(4,128)S(1)}, f32[16,3,768]{2,1,0:T(4,128)S(1)}, ...), condition=%wide.region_47.48_spmd.clone, body=%wide.region_43.47_spmd.clone.sunk | while | flops 21235968 | bytes 19003480 | solution.py:76
  488.8 6.0 psum.272
  494.8 9.4 %psum.273 = f32[3]{0:T(128)S(1)} all-reduce(f32[3]{0:T(128)S(1)} %psum.272), channel_id=1, replica_groups=mesh['wall_0'=4,'wall_1'=2,'cell_0'=4,'cell_1'=4] {'wall_1'}, use_global_device_ids=true, to_apply=%region_52.53 | all-reduce | flops 3 | bytes 24 | tf_op jit(solution)/shard_map/psum | solution.py:20
  504.2 8.8 psum.274
  513.0 8.4 psum.275
  522.1 2.6 multiply_reduce_fusion.5
  524.7 8.4 psum.276
  533.2 9.1 %psum.277 = f32[]{:T(128)} all-reduce(f32[]{:T(128)} %psum.276), channel_id=1, replica_groups=mesh['wall_0'=4,'wall_1'=2,'cell_0'=4,'cell_1'=4] {'wall_1'}, use_global_device_ids=true, to_apply=%region_57.58 | all-reduce | flops 1 | bytes 8 | tf_op jit(solution)/shard_map/psum | solution.py:20
  542.6 6.7 psum.278
  549.6 6.6 psum.279
  557.7 4.2 all-to-all-start.4
  561.9 47.1 %while.87 = (s32[]{:T(128)}, f32[2,3,544]{2,0,1:T(2,128)S(1)}, f32[2,3,544]{2,1,0:T(4,128)S(1)}, f32[2,8,6,544]{3,1,2,0:T(8,128)S(1)}, f32[2,3,544]{2,1,0:T(4,12...) while((s32[]{:T(128)}, f32[2,3,544]{2,0,1:T(2,128)S(1)}, f32[2,3,544]{2,1,0:T(4,128)S(1)}, ...), condition=%wide.region_6.7_spmd, body=%wide.region_0.6_spmd.sunk | while | flops 10684709 | bytes 10475524 | solution.py:144
  562.1 23.2 %while.94 = (s32[]{:T(128)}, f32[3,544]{1,0:T(4,128)S(1)}, f32[3,544]{1,0:T(4,128)S(1)}, f32[9,3,544]{2,1,0:T(4,128)S(1)}, f32[9,3,544]{2,1,0:T(4,128)S(1)}, /*index=5*/s32[]{:T(128)}, s32[]{:T(128)}) while((s32[]{:T(128)}, f32[3,544]{1,0:T(4,128)S(1)}, f32[3,544]{1,0:T(4,128)S(1)}, f32[9,3,544]{2,1,0:T(4,128)S(1)}, ...), condition=%wide.region_5.5_spmd.clone, body=%wide.region_1.4_spmd.clone.sunk | while | flops 10655331 | bytes 9561435 | solution.py:89
  585.7 23.2 %while.94 = (s32[]{:T(128)}, f32[3,544]{1,0:T(4,128)S(1)}, f32[3,544]{1,0:T(4,128)S(1)}, f32[9,3,544]{2,1,0:T(4,128)S(1)}, f32[9,3,544]{2,1,0:T(4,128)S(1)}, /*index=5*/s32[]{:T(128)}, s32[]{:T(128)}) while((s32[]{:T(128)}, f32[3,544]{1,0:T(4,128)S(1)}, f32[3,544]{1,0:T(4,128)S(1)}, f32[9,3,544]{2,1,0:T(4,128)S(1)}, ...), condition=%wide.region_5.5_spmd.clone, body=%wide.region_1.4_spmd.clone.sunk | while | flops 10655331 | bytes 9561435 | solution.py:89
  615.9 82.6 %while.93 = (s32[]{:T(128)}, f32[3,768]{1,0:T(4,128)S(1)}, f32[3,768]{1,0:T(4,128)S(1)}, f32[16,3,768]{2,1,0:T(4,128)S(1)}, f32[16,3,768]{2,1,0:T(4,128)S(1)}, /*index=5*/s32[]{:T(128)}, s32[]{:T(128)}) while((s32[]{:T(128)}, f32[3,768]{1,0:T(4,128)S(1)}, f32[3,768]{1,0:T(4,128)S(1)}, f32[16,3,768]{2,1,0:T(4,128)S(1)}, ...), condition=%wide.region_64.65_spmd.clone, body=%wide.region_60.64_spmd.clone.sunk | while | flops 21235968 | bytes 19003480 | solution.py:76
  699.2 2.6 pad_maximum_fusion.10
  701.8 6.0 psum.280
  707.8 8.2 psum.281
  716.0 8.8 psum.282
  724.8 8.4 psum.283
  735.7 3.2 multiply_reduce_fusion
  741.5 8.5 psum.284
  749.9 9.1 %psum.285 = f32[]{:T(128)} all-reduce(f32[]{:T(128)} %psum.284), channel_id=1, replica_groups=mesh['wall_0'=4,'wall_1'=2,'cell_0'=4,'cell_1'=4] {'wall_1'}, use_global_device_ids=true, to_apply=%region_75.76 | all-reduce | flops 1 | bytes 8 | tf_op jit(solution)/shard_map/psum | solution.py:20
  759.7 6.7 psum.286
  766.5 6.6 psum.287
  774.7 17.4 %all_gather.3 = f32[6,12288]{1,0:T(8,128)S(1)} all-gather(f32[6,768]{1,0:T(8,128)S(1)} %pad_maximum_fusion.6), channel_id=1, replica_groups=mesh['wall_0'=4,'wall_1'=2,'cell_0'=4,'cell_1'=4] {'cell_0','cell_1'}, dimensions={1}, use_global_device_ids=true | all-gather | bytes 313344 | tf_op jit(solution)/shard_map/all_gather | solution.py:52
  792.3 100.9 %while.89 = (s32[]{:T(128)}, f32[2,3,544]{2,0,1:T(2,128)S(1)}, f32[3,12288]{1,0:T(4,128)S(1)}, f32[3,12288]{1,0:T(4,128)S(1)}, f32[2,3,544]{2,1,0:T(4,128)S(1)},...) while((s32[]{:T(128)}, f32[2,3,544]{2,0,1:T(2,128)S(1)}, f32[3,12288]{1,0:T(4,128)S(1)}, ...), condition=%wide.region_84.85_spmd, body=%wide.region_78.84_spmd.sunk | while | flops 15042149 | bytes 13521664 | solution.py:175
  792.3 50.3 %while.95 = (s32[]{:T(128)}, f32[3,544]{1,0:T(4,128)S(1)}, f32[3,544]{1,0:T(4,128)S(1)}, f32[16,3,768]{2,1,0:T(4,128)S(1)}, f32[16,3,768]{2,1,0:T(4,128)S(1)}, /*index=5*/s32[]{:T(128)}, s32[]{:T(128)}) while((s32[]{:T(128)}, f32[3,544]{1,0:T(4,128)S(1)}, f32[3,544]{1,0:T(4,128)S(1)}, f32[16,3,768]{2,1,0:T(4,128)S(1)}, ...), condition=%wide.region_83.83_spmd.clone, body=%wide.region_79.82_spmd.clone.sunk | while | flops 15042147 | bytes 13482331 | solution.py:76
  842.7 50.3 %while.95 = (s32[]{:T(128)}, f32[3,544]{1,0:T(4,128)S(1)}, f32[3,544]{1,0:T(4,128)S(1)}, f32[16,3,768]{2,1,0:T(4,128)S(1)}, f32[16,3,768]{2,1,0:T(4,128)S(1)}, /*index=5*/s32[]{:T(128)}, s32[]{:T(128)}) while((s32[]{:T(128)}, f32[3,544]{1,0:T(4,128)S(1)}, f32[3,544]{1,0:T(4,128)S(1)}, f32[16,3,768]{2,1,0:T(4,128)S(1)}, ...), condition=%wide.region_83.83_spmd.clone, body=%wide.region_79.82_spmd.clone.sunk | while | flops 15042147 | bytes 13482331 | solution.py:76
  (717 shorter events, 503.4 us)
Async XLA Ops:
  39.9 11.5 %all-to-all-start.1 = ((f32[16,6,768]{2,1,0:T(8,128)}), f32[16,6,768]{2,1,0:T(8,128)S(1)}, u32[]{:S(2)}, u32[]{:S(2)}) async-start(f32[16,6,768]{2,1,0:T(8,128)} %broadcast_in_dim.27), calls=%async_computation.1 | async-start | bytes 786432 | tf_op jit(solution)/shard_map/all_to_all | solution.py:26
  51.4 94.3 %copy-start.3 = (f32[3,768]{1,0:T(4,128)S(1)}, f32[3,768]{1,0:T(4,128)}, u32[]{:S(2)}) copy-start(f32[3,768]{1,0:T(4,128)} %param.29) | copy-start | bytes 27652
  51.4 160.3 %copy-start.4 = (f32[768]{0:T(1024)S(1)}, f32[768]{0:T(1024)}, u32[]{:S(2)}) copy-start(f32[768]{0:T(1024)} %param.28) | copy-start | bytes 9220
  54.0 0.9 copy-start
  59.9 0.9 copy-start
  65.8 0.9 copy-start
  71.6 0.9 copy-start
  77.5 0.9 copy-start
  83.4 0.9 copy-start
  89.3 0.9 copy-start
  95.2 0.9 copy-start
  101.1 0.9 copy-start
  107.0 0.9 copy-start
  112.9 0.9 copy-start
  118.8 0.9 copy-start
  124.7 0.9 copy-start
  130.6 0.9 copy-start
  136.5 0.9 copy-start
  142.4 0.9 copy-start
  213.9 11.5 %all-to-all-start.2 = ((f32[16,6,768]{2,1,0:T(8,128)}), f32[16,6,768]{2,1,0:T(8,128)S(1)}, u32[]{:S(2)}, u32[]{:S(2)}) async-start(f32[16,6,768]{2,1,0:T(8,128)} %broadcast_in_dim.28), calls=%async_computation.2 | async-start | bytes 786432 | tf_op jit(solution)/shard_map/all_to_all | solution.py:26
  225.4 152.5 %copy-start.5 = (f32[2,3,544]{2,0,1:T(2,128)S(1)}, f32[2,3,544]{2,0,1:T(2,128)}, u32[]{:S(2)}) copy-start(f32[2,3,544]{2,0,1:T(2,128)} %param.23) | copy-start | bytes 39172
  225.5 165.4 %copy-start.6 = (f32[2,3,544]{2,0,1:T(2,128)S(1)}, f32[2,3,544]{2,0,1:T(2,128)}, u32[]{:S(2)}) copy-start(f32[2,3,544]{2,0,1:T(2,128)} %param.24) | copy-start | bytes 39172
  225.5 165.4 %copy-start.7 = (f32[2,544]{1,0:T(2,128)S(1)}, f32[2,544]{1,0:T(2,128)}, u32[]{:S(2)}) copy-start(f32[2,544]{1,0:T(2,128)} %param.25) | copy-start | bytes 13060
  228.0 0.9 copy-start.1
  233.9 0.9 copy-start.1
  239.8 0.9 copy-start.1
  245.7 0.9 copy-start.1
  251.6 0.9 copy-start.1
  257.5 0.9 copy-start.1
  263.4 0.9 copy-start.1
  269.2 0.9 copy-start.1
  275.1 0.9 copy-start.1
  281.0 0.9 copy-start.1
  286.9 0.9 copy-start.1
  292.8 0.9 copy-start.1
  298.7 0.9 copy-start.1
  304.6 0.9 copy-start.1
  310.5 0.9 copy-start.1
  316.4 0.9 copy-start.1
  319.8 83.8 %copy-start.2 = (f32[3,768]{1,0:T(4,128)S(1)}, f32[3,768]{1,0:T(4,128)}, u32[]{:S(2)}) copy-start(f32[3,768]{1,0:T(4,128)} %get-tuple-element.1063) | copy-start | bytes 27652
  387.3 11.5 %all-to-all-start.3 = ((f32[16,6,768]{2,1,0:T(8,128)}), f32[16,6,768]{2,1,0:T(8,128)S(1)}, u32[]{:S(2)}, u32[]{:S(2)}) async-start(f32[16,6,768]{2,1,0:T(8,128)} %broadcast_in_dim.29), calls=%async_computation.3 | async-start | bytes 786432 | tf_op jit(solution)/shard_map/all_to_all | solution.py:26
  399.7 113.2 %all-to-all-start = ((f32[16,2,6,544]{3,1,2,0:T(2,128)}), f32[16,2,6,544]{3,1,2,0:T(2,128)S(1)}, u32[]{:S(2)}, u32[]{:S(2)}) async-start(f32[16,2,6,544]{3,1,2,0:T(2,128)} %broadcast_in_dim.26), calls=%async_computation | async-start | bytes 983040 | tf_op jit(solution)/shard_map/all_to_all | solution.py:26
  486.2 63.1 %copy-start.8 = (s32[2,8]{1,0:T(2,128)S(1)}, s32[2,8]{1,0:T(2,128)}, u32[]{:S(2)}) copy-start(s32[2,8]{1,0:T(2,128)} %param.26) | copy-start | bytes 196
  557.7 58.1 %all-to-all-start.4 = ((f32[16,6,768]{2,1,0:T(8,128)}), f32[16,6,768]{2,1,0:T(8,128)S(1)}, u32[]{:S(2)}, u32[]{:S(2)}) async-start(f32[16,6,768]{2,1,0:T(8,128)} %broadcast_in_dim.30), calls=%async_computation.4 | async-start | bytes 786432 | tf_op jit(solution)/shard_map/all_to_all | solution.py:26
where the time goes:
time: 906 us; the launch traced here: 894 us
  other arithmetic  517 us (57%)
  blocking collectives  302 us (33%)
  waiting for transfers between devices  21.7 us (2%)
  starting transfers between devices  18.6 us (2%)
  between operations  18.6 us (2%)
    psum x36, blocking collectives, one_axis_at_a_time(): x = lax.psum(x, axis)  285 us
    reduce_sum x114, other arithmetic, stokeslet(): return jnp.sum(factor[None] * terms, axis=2)  226 us
    reduce_sum x114, other arithmetic, stokeslet(): square_dist = jnp.sum(offsets * offsets, axis=0)  176 us
    div x114, other arithmetic, stokeslet(): factor = 1.0 / (8.0 * math.pi * shifted * jnp.sqrt(shifted))  90 us
    all_to_all x5, waiting for transfers between devices, from_everyone(): lax.all_to_all(jnp.broadcast_to(x[None], (length, *x.shape)), axis, 0, 0,...  21.7 us
    all_to_all x5, starting transfers between devices, from_everyone(): lax.all_to_all(jnp.broadcast_to(x[None], (length, *x.shape)), axis, 0, 0,...  18.6 us
  transfers between devices with their start and end apart: 5, of which 3 were waited for; matrix products, arithmetic and copies ran while one was open for 15% of the time, Pallas kernels for 0%

commit v1 on v0

v1 whole, which is shorter than its diff:
```python
import math

import jax
import jax.numpy as jnp
from jax import lax
from jax.experimental import pallas as pl
from jax.experimental.pallas import tpu as pltpu
from jax.sharding import PartitionSpec as P

F32 = jnp.float32
BF16 = jnp.bfloat16
AXES = ("wall", "cell")
E2 = 0.1 * 0.1
FLOOR = 1e-06
SCALE = 1.0 / (8.0 * math.pi)
VMEM_LIMIT = 48 * 2**20


def row_of(n):
    return lax.broadcasted_iota(jnp.int32, (8, n), 0)


def split3(a):
    high = a.astype(BF16).astype(F32)
    rest = a - high
    mid = rest.astype(BF16).astype(F32)
    low = (rest - mid).astype(BF16).astype(F32)
    return high, mid, low


def target_rows(points):
    n = points.shape[1]
    row = row_of(n)
    coords = jnp.where(row < 3, points, 0.0)
    norm2 = jnp.sum(coords * coords, axis=0, keepdims=True) + E2
    eight = jnp.where(row < 3, -2.0 * coords, jnp.where(row == 3, 1.0, jnp.where(row == 4, norm2, 0.0)))
    h, m, l = split3(eight)
    wide = jnp.concatenate([h, m, l, h, m, h] + [jnp.zeros_like(h)] * 10, axis=0)
    return jnp.transpose(wide)[:, :48].astype(BF16)


def source_columns(points):
    n = points.shape[1]
    row = row_of(n)
    coords = jnp.where(row < 3, points, 0.0)
    norm2 = jnp.sum(coords * coords, axis=0, keepdims=True)
    eight = jnp.where(row < 3, coords, jnp.where(row == 3, norm2, jnp.where(row == 4, 1.0, 0.0)))
    h, m, l = split3(eight)
    return jnp.concatenate([h, h, h, m, m, l], axis=0).astype(BF16)


def moment_rows(points, twice):
    n = points.shape[1]
    row = row_of(n)
    coords = jnp.where(row < 3, points, 0.0)
    y0, y1, y2 = points[0:1], points[1:2], points[2:3]
    norm2 = jnp.sum(coords * coords, axis=0, keepdims=True)
    inner = jnp.sum(coords * twice, axis=0, keepdims=True)
    first = twice * jnp.where(row < 4, 1.0, y0)
    second = twice * jnp.where(row < 4, y1, y2)
    third = jnp.where(row < 4, norm2 * twice + inner * coords, 0.0)
    return first, second, third


def moment_block(blocks):
    parts = [split3(b) for b in blocks]
    rows = [p[k] for k in range(3) for p in parts]
    return jnp.concatenate(rows, axis=0).astype(BF16)


def accumulate(acc, left, right, moments, blocks, hilo):
    dims = (((1,), (1,)), ((), ()))
    for start, size in blocks:
        shifted = jnp.dot(left[start : start + size, :], right, preferred_element_type=F32)
        inv = lax.rsqrt(shifted)
        kern = inv * inv * inv
        high = kern.astype(BF16)
        term = lax.dot_general(high, moments, dims, preferred_element_type=F32)
        if hilo:
            low = (kern - high.astype(F32)).astype(BF16)
            term = term + lax.dot_general(low, moments, dims, preferred_element_type=F32)
        acc[start : start + size, : term.shape[1]] += term


def assemble(points, f, t0, t1, t2, e):
    n = points.shape[1]
    row = lax.broadcasted_iota(jnp.int32, (4, n), 0)
    x4 = jnp.where(row < 3, points[0:4], 0.0)
    x0, x1, x2 = x4[0:1], x4[1:2], x4[2:3]
    norm2 = jnp.sum(x4 * x4, axis=0, keepdims=True)
    along = jnp.sum(x4 * f, axis=0, keepdims=True) - (t0[0:1] + t1[1:2] + t2[2:3])
    s0 = jnp.sum(x4 * t0, axis=0, keepdims=True)
    s1 = jnp.sum(x4 * t1, axis=0, keepdims=True)
    s2 = jnp.sum(x4 * t2, axis=0, keepdims=True)
    cross = jnp.where(row == 0, s0, jnp.where(row == 1, s1, jnp.where(row == 2, s2, 0.0)))
    return (norm2 + 2.0 * E2) * f + e - 2.0 * (x0 * t0 + x1 * t1 + x2 * t2) + x4 * along - cross


def velocity(points, acc):
    rows = jnp.transpose(acc)
    rows = rows[0:24] + rows[24:48] + rows[48:72]
    return assemble(points, rows[0:4], rows[4:8], rows[8:12], rows[12:16], rows[16:20])


def scalars(reds):
    first = reds[0]
    beta2 = first[0] + FLOOR
    beta = jnp.sqrt(beta2)
    g = {(0, 0): first[0] / beta2}
    hess = {}
    comb = []
    for j in range(len(reds)):
        if j == 0:
            b, ss = [first[1] / beta2], first[2] / beta2
        else:
            b, ss = reds[j][:-1], reds[j][-1]
        gram = lambda p, q: g[(min(p, q), max(p, q))]
        c = []
        for i in range(j + 1):
            h = 0.5 * gram(i, j) + b[i]
            for k in range(i):
                h = h - hess[(k, j)] * gram(k, i)
            hess[(i, j)] = h
            c.append(h - 0.5 if i == j else h)
        norm2 = ss
        for i in range(j + 1):
            norm2 = norm2 - 2.0 * c[i] * b[i]
            for k in range(j + 1):
                norm2 = norm2 + c[i] * c[k] * gram(i, k)
        norm2 = jnp.maximum(norm2, 0.0)
        h = jnp.sqrt(norm2 + FLOOR)
        hess[(j + 1, j)] = h
        for i in range(j + 1):
            v = b[i]
            for k in range(j + 1):
                v = v - c[k] * gram(i, k)
            g[(i, j + 1)] = v / h
        g[(j + 1, j + 1)] = norm2 / (h * h)
        comb.append((c, h))
    return beta, hess, comb


def solve_small(hess, beta, size):
    zero = jnp.zeros_like(beta)
    upper = [[hess.get((r, c), zero) for c in range(size)] for r in range(size + 1)]
    targets = [beta] + [zero] * size
    cosines, sines = [], []
    for column in range(size):
        for prior in range(column):
            a, b = upper[prior][column], upper[prior + 1][column]
            upper[prior][column] = cosines[prior] * a + sines[prior] * b
            upper[prior + 1][column] = cosines[prior] * b - sines[prior] * a
        a, b = upper[column][column], upper[column + 1][column]
        radius = jnp.sqrt(a * a + b * b)
        cosines.append(a / radius)
        sines.append(b / radius)
        upper[column][column] = radius
        targets[column + 1] = -sines[column] * targets[column]
        targets[column] = cosines[column] * targets[column]
    weights = [None] * size
    for column in reversed(range(size)):
        part = targets[column]
        for later in range(column + 1, size):
            part = part - upper[column][later] * weights[later]
        weights[column] = part / upper[column][column]
    return weights


def red_rows(ref, count):
    total = jnp.sum(ref[...], axis=0)
    return [total[k : k + 1, 0:1] for k in range(count)]


def put_sums(out, values):
    row = lax.broadcasted_iota(jnp.int32, (8, 128), 0)
    tile = jnp.zeros((8, 128), F32)
    for k, v in enumerate(values):
        tile = jnp.where(row == k, jnp.broadcast_to(v, (8, 128)), tile)
    for p in range(out.shape[0]):
        out[p] = tile


def total(a):
    while a.ndim > 2:
        a = jnp.sum(a, axis=0)
    return jnp.sum(jnp.sum(a, axis=0, keepdims=True), axis=1, keepdims=True)


def call(body, outs, ins, name, scratch=(), smem=()):
    specs = [pl.BlockSpec(memory_space=pltpu.SMEM if k in smem else pltpu.VMEM) for k in range(len(ins))]
    many = isinstance(outs, (list, tuple))
    ospec = pl.BlockSpec(memory_space=pltpu.VMEM)
    return pl.pallas_call(
        body,
        out_shape=outs,
        in_specs=specs,
        out_specs=[ospec] * len(outs) if many else ospec,
        scratch_shapes=list(scratch),
        compiler_params=pltpu.CompilerParams(vmem_limit_bytes=VMEM_LIMIT),
        name=name,
    )(*ins)


def shape(*dims, dtype=F32):
    return jax.ShapeDtypeStruct(dims, dtype)


def blocks_of(n, size):
    return [(k * size, size) for k in range(n // size)]


def near_body(partners, own, everyone, out, left, acc, sources):
    cells = own.shape[0]
    width = own.shape[2]
    slots = partners.shape[1]
    used = out.shape[2]
    row = row_of(width)

    def one(i, _):
        mine = own[i]
        centre = jnp.where(row < 3, mine[:, 0:1], 0.0)
        sources[:, 0:width] = mine - centre
        for k in range(slots):
            n = partners[i, k]
            there = jnp.maximum(n, 0)
            other = everyone[there // cells, there % cells] - centre
            keep = jnp.where(n >= 0, 1.0, 0.0)
            sources[:, (k + 1) * width : (k + 2) * width] = jnp.where(row >= 4, other * keep, other)
        sources[:, (slots + 1) * width :] = jnp.zeros((8, width), F32)
        left[...] = target_rows(mine - centre)
        acc[...] = jnp.zeros_like(acc)

        def step(s, _):
            pts = sources[:, pl.ds(pl.multiple_of(s * 2 * width, 2 * width), 2 * width)]
            r = row_of(2 * width)
            twice = SCALE * jnp.where(r >= 4, pts, pltpu.roll(pts, 4, 0))
            moments = moment_block(moment_rows(pts, twice))
            accumulate(acc, left, source_columns(pts), moments, blocks_of(used, used // 2), True)
            return 0

        lax.fori_loop(0, (slots + 2) // 2, step, 0)
        vel = velocity(mine - centre, acc[...])
        out[i] = vel[0:3, :used]
        return 0

    lax.fori_loop(0, cells, one, 0)


def first_body(mine, group, right, out, left, acc):
    n = mine.shape[1]
    left[...] = target_rows(mine[...])
    acc[...] = jnp.zeros_like(acc)
    row = row_of(n)

    def step(s, _):
        pts = group[s]
        cols = source_columns(pts)
        right[s] = cols
        area = SCALE * pts[3:4]
        twice = area * jnp.where(row >= 4, pts, pltpu.roll(pts, 4, 0))
        moments = moment_block(moment_rows(pts, twice))
        accumulate(acc, left, cols, moments, blocks_of(n, 256), HILO)
        return 0

    lax.fori_loop(0, group.shape[0], step, 0)
    vel = velocity(mine[...], acc[...])
    for p in range(out.shape[0]):
        out[p] = vel


def apply_body(mine, group, right, vector, out, left, acc):
    n = mine.shape[1]
    left[...] = target_rows(mine[...])
    acc[...] = jnp.zeros_like(acc)

    def step(s, _):
        pts = group[s]
        four = vector[s] * (SCALE * pts[3:4])
        moments = moment_block(moment_rows(pts, jnp.concatenate([four, four], axis=0)))
        accumulate(acc, left, right[s], moments, blocks_of(n, 256), HILO)
        return 0

    lax.fori_loop(0, group.shape[0], step, 0)
    out[...] = velocity(mine[...], acc[...])


def data_rows(block):
    return block[:, 4:8, :]


def pre1_body(group, u0, out):
    d = data_rows(group[...])
    u = u0[...]
    put_sums(out, [total(d * d), total(u * d), total(u * u)])


def pre2_body(red1, group, u0, s1, v1, out):
    beta, _, comb = scalars([red_rows(red1, 3)])
    (c,), h = comb[0]
    v0 = data_rows(group[...]) / beta
    one = (u0[...] / beta - c * v0) / h
    v1[...] = one
    s = s1[...]
    put_sums(out, [total(s * v0), total(s * one), total(s * s)])


def pre3_body(red1, red2, group, v1, s1, s2, v2, out):
    beta, _, comb = scalars([red_rows(red1, 3), red_rows(red2, 3)])
    (c0, c1), h = comb[1]
    v0 = data_rows(group[...]) / beta
    one = v1[...]
    two = (s1[...] - c0 * v0 - c1 * one) / h
    v2[...] = two
    s = s2[...]
    put_sums(out, [total(s * v0), total(s * one), total(s * two), total(s * s)])


def post1_body(red1, u0, t1, out):
    beta, _, comb = scalars([red_rows(red1, 3)])
    (c,), h = comb[0]
    s0 = u0[0] / beta
    s1 = (t1[...] / beta - c * s0) / h
    for p in range(out.shape[0]):
        out[p] = s1


def post2_body(red1, red2, u0, s1, t2, out):
    beta, _, comb = scalars([red_rows(red1, 3), red_rows(red2, 3)])
    (c0, c1), h = comb[1]
    s2 = (t2[...] - c0 * (u0[0] / beta) - c1 * s1[0]) / h
    for p in range(out.shape[0]):
        out[p] = s2


def post3_body(red1, red2, red3, mine, u0, s1, s2, t3, basis, out):
    beta, _, comb = scalars([red_rows(red1, 3), red_rows(red2, 3), red_rows(red3, 4)])
    (b0,), h1 = comb[0]
    (c0, c1), h2 = comb[1]
    (d0, d1, d2), h3 = comb[2]
    v0 = mine[4:8] / beta
    s0 = u0[0] / beta
    v1 = (s0 - b0 * v0) / h1
    v2 = (s1[0] - c0 * v0 - c1 * v1) / h2
    v3 = (s2[0] - d0 * v0 - d1 * v1 - d2 * v2) / h3
    s3 = (t3[...] - d0 * s0 - d1 * s1[0] - d2 * s2[0]) / h3
    for k, v in enumerate([v0, v1, v2, v3]):
        basis[k] = v
    put_sums(out, [total(s3 * v) for v in (v0, v1, v2, v3)] + [total(s3 * s3)])


def cells_body(centre, red1, red2, red3, own, group, right, v1, v2, s2, out, left, acc):
    beta, _, comb = scalars([red_rows(red1, 3), red_rows(red2, 3), red_rows(red3, 4)])
    (d0, d1, d2), h3 = comb[2]
    cells = own.shape[0]
    used = out.shape[3]
    width = own.shape[2]
    row = row_of(width)
    shift = jnp.where(row == 0, centre[0], 0.0)
    for i in range(cells):
        left[i * used : (i + 1) * used, :] = target_rows(own[i] - shift)[:used]
    acc[...] = jnp.zeros_like(acc)

    def step(s, _):
        pts = group[s]
        area = SCALE * pts[3:4]
        v0 = pts[4:8] / beta
        a1, a2 = v1[s], v2[s]
        a3 = (s2[s] - d0 * v0 - d1 * a1 - d2 * a2) / h3
        rows = []
        for pair in ((v0, a1), (a2, a3)):
            thirds = []
            for v in pair:
                four = area * v
                p, q, t = moment_rows(pts, jnp.concatenate([four, four], axis=0))
                rows += [p, q]
                thirds.append(t)
            rows.append(thirds[0] + pltpu.roll(thirds[1], 4, 0))
        accumulate(acc, left, right[s], moment_block(rows), blocks_of(cells * used, used // 2), HILO_CELLS)
        return 0

    lax.fori_loop(0, group.shape[0], step, 0)
    for i in range(cells):
        pts = own[i] - shift
        full = jnp.concatenate([acc[i * used : (i + 1) * used, :], jnp.zeros((width - used, 256), F32)], axis=0)
        rows = jnp.transpose(full)
        rows = rows[0:80] + rows[80:160] + rows[160:240]
        for k in range(4):
            at, half = 40 * (k // 2), k % 2
            p, q = rows[at + 16 * half : at + 16 * half + 8], rows[at + 16 * half + 8 : at + 16 * half + 16]
            e = rows[at + 32 + 4 * half : at + 36 + 4 * half]
            vel = assemble(pts, p[0:4], p[4:8], q[0:4], q[4:8], e)
            out[k, i] = vel[0:3, :used]


def last_body(red1, red2, red3, red4, basis, near, wall, velocity_out, density_out):
    reds = [red_rows(red1, 3), red_rows(red2, 3), red_rows(red3, 4), red_rows(red4, 5)]
    beta, hess, _ = scalars(reds)
    y = solve_small(hess, beta, 4)
    density = y[0] * basis[0]
    for k in range(1, 4):
        density = density + y[k] * basis[k]
    density_out[...] = density[0:3]
    for i in range(near.shape[0]):
        part = y[0] * wall[0, i]
        for k in range(1, 4):
            part = part + y[k] * wall[k, i]
        velocity_out[i] = near[i] + part


HILO = True
HILO_CELLS = True


def swap(x, axes):
    return lax.all_to_all(x, axes, 0, 0, tiled=True)


def per_device(cell_points, cell_force, cell_weight, partners, wall_points, wall_area, wall_data):
    cells, _, surface = cell_points.shape
    points = wall_points.shape[1]
    segments, peers = lax.axis_size("wall"), lax.axis_size("cell")
    width = -(-surface // 128) * 128
    centre = 8.0 * lax.axis_index("wall").astype(F32) + 4.0

    strength = cell_force * cell_weight[:, None, :]
    gap = jnp.zeros((cells, 1, surface), F32)
    own = jnp.concatenate([cell_points, gap, strength, gap], axis=1)
    own = jnp.pad(own, ((0, 0), (0, 0), (0, width - surface)))
    shift = jnp.stack([centre, jnp.zeros_like(centre), jnp.zeros_like(centre)])
    mine = jnp.concatenate(
        [wall_points - shift[:, None], wall_area[None], wall_data, jnp.zeros((1, points), F32)], axis=0
    )
    group = swap(jnp.broadcast_to(mine[None], (peers, *mine.shape)), "cell")
    everyone = swap(jnp.broadcast_to(own[None], (peers, *own.shape)), "cell")

    wall_scratch = (pltpu.VMEM((points, 48), BF16), pltpu.VMEM((points, 128), F32))
    copies = shape(peers, 4, points)
    sums = shape(segments, 8, 128)

    right, u0 = call(
        first_body, [shape(peers, 48, points, dtype=BF16), copies], (mine, group), "first", wall_scratch
    )
    u0_all = swap(u0, "cell")
    near = call(
        near_body,
        shape(cells, 3, surface),
        (partners, own, everyone),
        "near",
        (
            pltpu.VMEM((width, 48), BF16),
            pltpu.VMEM((width, 128), F32),
            pltpu.VMEM((8, (partners.shape[1] + 2) * width), F32),
        ),
        smem=(0,),
    )

    def apply(vector):
        return call(apply_body, shape(4, points), (mine, group, right, vector), "apply", wall_scratch)

    red1 = swap(call(pre1_body, sums, (group, u0_all), "pre1"), "wall")
    t1 = apply(u0_all)
    s1 = call(post1_body, copies, (red1, u0, t1), "post1")
    s1_all = swap(s1, "cell")
    v1, sum2 = call(pre2_body, [copies, sums], (red1, group, u0_all, s1_all), "pre2")
    red2 = swap(sum2, "wall")
    t2 = apply(s1_all)
    s2 = call(post2_body, copies, (red1, red2, u0, s1, t2), "post2")
    s2_all = swap(s2, "cell")
    v2, sum3 = call(pre3_body, [copies, sums], (red1, red2, group, v1, s1_all, s2_all), "pre3")
    red3 = swap(sum3, "wall")
    t3 = apply(s2_all)
    basis, sum4 = call(
        post3_body,
        [shape(4, 4, points), shape(segments * peers, 8, 128)],
        (red1, red2, red3, mine, u0, s1, s2, t3),
        "post3",
    )
    red4 = swap(sum4, AXES)
    wall = call(
        cells_body,
        shape(4, cells, 3, surface),
        (centre[None], red1, red2, red3, own, group, right, v1, v2, s2_all),
        "cells",
        (pltpu.VMEM((cells * surface, 48), BF16), pltpu.VMEM((cells * surface, 256), F32)),
        smem=(0,),
    )
    velocity_out, density = call(
        last_body,
        [shape(cells, 3, surface), shape(3, points)],
        (red1, red2, red3, red4, basis, near, wall),
        "last",
    )
    return velocity_out, density


def solution(mesh):
    in_specs = (
        P(AXES, None, None),
        P(AXES, None, None),
        P(AXES, None),
        P(AXES, None),
        P(None, AXES),
        P(AXES),
        P(None, AXES),
    )
    out_specs = (P(AXES, None, None), P(None, AXES))
    return jax.shard_map(per_device, mesh=mesh, in_specs=in_specs, out_specs=out_specs, check_vma=False)
```

time: 906 us -> 226 us (0.25); the launches traced: 894 us -> 225 us
  other arithmetic: 517 us -> 1.59 us
  blocking collectives: 302 us -> 37.9 us
  Pallas kernels: 0 us -> 133 us
  between operations: 18.6 us -> 0.89 us
  starting transfers between devices: 18.6 us -> 34.7 us
  waiting for transfers between devices: 21.7 us -> 12 us
    reduce_sum x237 -> x0, other arithmetic: 415 us -> none  [the longest x114 226 us: stokeslet(): return jnp.sum(factor[None] * terms, axis=2)]
    psum x36 -> x0, blocking collectives: 285 us -> none  [one_axis_at_a_time(): x = lax.psum(x, axis)]
    pallas_call x0 -> x13, Pallas kernels: none -> 133 us  [call(): pl.pallas_call(body, out_shape=outs, in_specs=specs, out_specs=[ospec] *...]
    div x114 -> x0, other arithmetic: 90 us -> none  [stokeslet(): factor = 1.0 / (8.0 * math.pi * shifted * jnp.sqrt(shifted))]
    all_to_all x0 -> x3, blocking collectives: none -> 37.9 us  [swap(): return lax.all_to_all(x, axes, 0, 0, tiled=True)]
    all_gather x1 -> x0, blocking collectives: 17.4 us -> none  [sent_together_2(): out = lax.all_gather(both, axis, axis=dim, tiled=True)]
    all_to_all x5 -> x6, starting transfers between devices: 18.6 us -> 34.7 us  [swap(): return lax.all_to_all(x, axes, 0, 0, tiled=True)]
    all_to_all x5 -> x6, waiting for transfers between devices: 21.7 us -> 12 us  [swap(): return lax.all_to_all(x, axes, 0, 0, tiled=True)]
  transfers between devices with their start and end apart: 5 -> 6, of which waited for: 3 -> 2; matrix products, arithmetic and copies ran while one was open for 15% -> 0% of each run, Pallas kernels for 0% -> 47%
where the time goes in v1:
time: 226 us; the launch traced here: 225 us
  Pallas kernels  133 us (59%)
  blocking collectives  37.9 us (17%)
  starting transfers between devices  34.7 us (15%)
  waiting for transfers between devices  12 us (5%)
  local copies, waits for them, and re-layouts  5.41 us (2%)
    pallas_call x13, Pallas kernels, call(): pl.pallas_call(body, out_shape=outs, in_specs=specs, out_specs=[ospec] *...  133 us
    all_to_all x3, blocking collectives, swap(): return lax.all_to_all(x, axes, 0, 0, tiled=True)  37.9 us
    all_to_all x6, starting transfers between devices, swap(): return lax.all_to_all(x, axes, 0, 0, tiled=True)  34.7 us
    all_to_all x6, waiting for transfers between devices, swap(): return lax.all_to_all(x, axes, 0, 0, tiled=True)  12 us
  transfers between devices with their start and end apart: 6, of which 2 were waited for; matrix products, arithmetic and copies ran while one was open for 0% of the time, Pallas kernels for 47%

profile of v1, /device:TPU:1, one launch (start us, length us, event | category | flops | bytes accessed | tf_op | source)
XLA Modules:
  0.0 225.0 jit_solution(14009550729455645732)
XLA Ops:
  0.6 0.7 broadcast_in_dim.10
  1.3 0.8 broadcast_subtract_fusion
  2.1 0.1 pad.13.clone
  2.2 0.8 maximum_maximum_fusion.mine
  3.0 16.5 %all_to_all.45.group = f32[16,8,768]{2,1,0:T(8,128)S(1)} all-to-all(f32[16,8,768]{2,1,0:T(8,128)S(1)} %broadcast_in_dim.12), channel_id=1, replica_groups=mesh['wall'=8,'cell'=16] {'cell'}, dimensions={0} | all-to-all | bytes 786432 | tf_op jit(solution)/shard_map/all_to_all | solution.py:415
  19.5 21.1 %first.1 = (bf16[16,48,768]{2,1,0:T(8,128)(2,1)S(1)}, f32[16,4,768]{2,1,0:T(4,128)S(1)}) custom-call(f32[8,768]{1,0:T(8,128)S(1)} %maximum_maximum_fusion.mine, f32[16,8,768]{2,1,0:T(8,128)S(1)} %all_to_all.45.group), custom_call_target="tpu_custom_call" | custom-call | tf_op jit(solution)/shard_map/first/pallas_call | solution.py:193
  40.6 11.0 %all_to_all.46.u0.vector = f32[16,4,768]{2,1,0:T(4,128)S(1)} all-to-all(f32[16,4,768]{2,1,0:T(4,128)S(1)} %get-tuple-element.10.u0), channel_id=1, replica_groups=mesh['wall'=8,'cell'=16] {'cell'}, dimensions={0} | all-to-all | bytes 393216 | tf_op jit(solution)/shard_map/all_to_all | solution.py:415
  51.6 0.9 pre1.1
  52.5 7.6 %all-to-all-start.2 = ((f32[8,8,128]{2,1,0:T(8,128)}), f32[8,8,128]{2,1,0:T(8,128)S(1)}, u32[]{:S(2)}, u32[]{:S(2)}) async-start(f32[8,8,128]{2,1,0:T(8,128)} %pre1.1), calls=%async_computation.2 | async-start | bytes 65536 | tf_op jit(solution)/shard_map/all_to_all | solution.py:415
  60.0 20.9 %apply.3.t1 = f32[4,768]{1,0:T(4,128)S(1)} custom-call(f32[8,768]{1,0:T(8,128)S(1)} %maximum_maximum_fusion.mine, f32[16,8,768]{2,1,0:T(8,128)S(1)} %all_to_all.45.group, bf16[16,48,768]{2,1,0:T(8,128)(2,1)S(1)} %get-tuple-element.11.right, f32[16,4,768]{2,1,0:T(4,128)S(1)} %all_to_all.46.u0.vector), custom_call_target="tpu_custom_call" | custom-call | tf_op jit(solution)/shard_map/apply/pallas_call | solution.py:193
  81.0 0.0 copy-start.10
  81.0 0.0 all-to-all-done.2.red1
  81.0 0.0 copy-start
  81.0 0.1 post1.1.s1
  81.1 10.4 %all_to_all.47.s1.vector = f32[16,4,768]{2,1,0:T(4,128)S(1)} all-to-all(f32[16,4,768]{2,1,0:T(4,128)S(1)} %post1.1.s1), channel_id=1, replica_groups=mesh['wall'=8,'cell'=16] {'cell'}, dimensions={0} | all-to-all | bytes 393216 | tf_op jit(solution)/shard_map/all_to_all | solution.py:415
  91.5 1.0 pre2.1
  92.5 0.0 copy-start.4
  92.5 6.1 %all-to-all-start.4 = ((f32[8,8,128]{2,1,0:T(8,128)}), f32[8,8,128]{2,1,0:T(8,128)S(1)}, u32[]{:S(2)}, u32[]{:S(2)}) async-start(f32[8,8,128]{2,1,0:T(8,128)} %get-tuple-element.12), calls=%async_computation.4 | async-start | bytes 65536 | tf_op jit(solution)/shard_map/all_to_all | solution.py:415
  98.6 0.0 copy-done.10
  98.6 0.0 copy-start.11
  98.7 0.0 copy-start.12
  98.7 20.9 %apply.4.t2 = f32[4,768]{1,0:T(4,128)S(1)} custom-call(f32[8,768]{1,0:T(8,128)S(1)} %maximum_maximum_fusion.mine, f32[16,8,768]{2,1,0:T(8,128)S(1)} %all_to_all.45.group, bf16[16,48,768]{2,1,0:T(8,128)(2,1)S(1)} %get-tuple-element.11.right, f32[16,4,768]{2,1,0:T(4,128)S(1)} %all_to_all.47.s1.vector), custom_call_target="tpu_custom_call" | custom-call | tf_op jit(solution)/shard_map/apply/pallas_call | solution.py:193
  119.6 0.0 all-to-all-done.4.red2
  119.6 0.0 copy-start.2
  119.6 0.8 post2.1.s2
  120.4 3.5 %all-to-all-start.5 = ((f32[16,4,768]{2,1,0:T(4,128)}), f32[16,4,768]{2,1,0:T(4,128)S(1)}, u32[]{:S(2)}, u32[]{:S(2)}) async-start(f32[16,4,768]{2,1,0:T(4,128)} %post2.1.s2), calls=%async_computation.5 | async-start | bytes 393216 | tf_op jit(solution)/shard_map/all_to_all | solution.py:415
  124.0 0.0 copy-done.11
  124.0 0.0 copy-done.12
  124.0 7.3 %all-to-all-done.5.s2.vector = f32[16,4,768]{2,1,0:T(4,128)S(1)} async-done(((f32[16,4,768]{2,1,0:T(4,128)}), f32[16,4,768]{2,1,0:T(4,128)S(1)}, u32[]{:S(2)}, u32[]{:S(2)}) %all-to-all-start.5) | async-done | bytes 196640 | tf_op jit(solution)/shard_map/all_to_all | solution.py:415
  131.3 0.0 copy-done.4
  131.3 1.1 pre3.1
  132.4 0.0 copy-start.7
  132.4 0.7 copy-done.7
  133.1 5.8 %all-to-all-start.6 = ((f32[8,8,128]{2,1,0:T(8,128)}), f32[8,8,128]{2,1,0:T(8,128)S(1)}, u32[]{:S(2)}, u32[]{:S(2)}) async-start(f32[8,8,128]{2,1,0:T(8,128)} %get-tuple-element.14), calls=%async_computation.6 | async-start | bytes 65536 | tf_op jit(solution)/shard_map/all_to_all | solution.py:415
  138.9 4.7 %all-to-all-done.6.red3 = f32[8,8,128]{2,1,0:T(8,128)S(1)} async-done(((f32[8,8,128]{2,1,0:T(8,128)}), f32[8,8,128]{2,1,0:T(8,128)S(1)}, u32[]{:S(2)}, u32[]{:S(2)}) %all-to-all-start.6) | async-done | bytes 32800 | tf_op jit(solution)/shard_map/all_to_all | solution.py:415
  143.6 0.9 broadcast_in_dim.28
  144.5 3.6 %all-to-all-start.8 = ((f32[16,2,8,640]{3,2,1,0:T(8,128)}), f32[16,2,8,640]{3,2,1,0:T(8,128)S(1)}, u32[]{:S(2)}, u32[]{:S(2)}) async-start(f32[16,2,8,640]{3,2,1,0:T(8,128)} %broadcast_in_dim.28), calls=%async_computation.8 | async-start | bytes 1310720 | tf_op jit(solution)/shard_map/all_to_all | solution.py:415
  148.1 21.0 %apply.5.t3 = f32[4,768]{1,0:T(4,128)S(1)} custom-call(f32[8,768]{1,0:T(8,128)S(1)} %maximum_maximum_fusion.mine, f32[16,8,768]{2,1,0:T(8,128)S(1)} %all_to_all.45.group, bf16[16,48,768]{2,1,0:T(8,128)(2,1)S(1)} %get-tuple-element.11.right, f32[16,4,768]{2,1,0:T(4,128)S(1)} %all-to-all-done.5.s2.vector), custom_call_target="tpu_custom_call" | custom-call | tf_op jit(solution)/shard_map/apply/pallas_call | solution.py:193
  169.1 0.0 copy-done
  169.1 0.0 copy-done.2
  169.1 1.2 post3.1
  170.3 0.0 copy-start.6
  170.4 0.8 copy-done.6
  171.2 0.0 copy-start.1
  171.2 0.0 copy-start.3
  171.2 0.0 copy-start.5
  171.2 0.0 all-to-all-done.8.everyone
  171.2 8.0 %all-to-all-start.7 = ((f32[128,8,128]{2,1,0:T(8,128)}), f32[128,8,128]{2,1,0:T(8,128)S(1)}, u32[]{:S(2)}, u32[]{:S(2)}) async-start(f32[128,8,128]{2,1,0:T(8,128)} %copy-done.6), calls=%async_computation.7 | async-start | bytes 1048576 | tf_op jit(solution)/shard_map/all_to_all | solution.py:415
  179.2 0.0 copy-start.9
  179.2 0.7 copy-done.9
  179.9 15.2 %near.1 = f32[2,3,544]{2,1,0:T(4,128)S(1)} custom-call(s32[2,8]{1,0:T(2,128)S(1)} %copy-done.9, f32[2,8,640]{2,1,0:T(8,128)S(1)} %select_maximum_fusion.own, f32[16,2,8,640]{3,2,1,0:T(8,128)S(1)} %all-to-all-done.8.everyone), custom_call_target="tpu_custom_call" | custom-call | tf_op jit(solution)/shard_map/near/pallas_call | solution.py:193
  195.1 0.0 copy-done.1
  195.1 0.0 copy-done.3
  195.1 0.0 copy-done.5
  195.1 0.0 copy-start.8
  195.1 0.9 copy-done.8
  196.0 27.5 %cells.1.wall = f32[4,2,3,544]{3,2,1,0:T(4,128)S(1)} custom-call(f32[1]{0:T(128)} %bitcast.centre, f32[8,8,128]{2,1,0:T(8,128)S(1)} %copy-done.1, f32[8,8,128]{2,1,0:T(8,128)S(1)} %copy-done.3, f32[8,8,128]{2,1,0:T(8,128)S(1)} %all-to-all-done.6.red3, f32[2,8,640]{2,1,0:T(8,128)S(1)} %select_maximum_fusion.own, f32[16,8,768]{2,1,0:T(8,128)S(1)} %all_to_all.45.group, ...), custom_call_target="tpu_custom_call" | custom-call | tf_op jit(solution)/shard_map/cells/pallas_call | solution.py:193
  223.5 0.0 all-to-all-done.7.red4
  223.5 0.9 last.1
  224.4 0.6 copy.11
  (6 shorter events, 0.1 us)
Async XLA Ops:
  52.5 28.5 %all-to-all-start.2 = ((f32[8,8,128]{2,1,0:T(8,128)}), f32[8,8,128]{2,1,0:T(8,128)S(1)}, u32[]{:S(2)}, u32[]{:S(2)}) async-start(f32[8,8,128]{2,1,0:T(8,128)} %pre1.1), calls=%async_computation.2 | async-start | bytes 65536 | tf_op jit(solution)/shard_map/all_to_all | solution.py:415
  81.0 17.7 %copy-start.10 = (f32[2,3,544]{2,0,1:T(2,128)S(1)}, f32[2,3,544]{2,0,1:T(2,128)}, u32[]{:S(2)}) copy-start(f32[2,3,544]{2,0,1:T(2,128)} %param.7) | copy-start | bytes 39172
  81.0 88.1 %copy-start = (f32[8,8,128]{2,1,0:T(8,128)}, f32[8,8,128]{2,1,0:T(8,128)S(1)}, u32[]{:S(2)}) copy-start(f32[8,8,128]{2,1,0:T(8,128)S(1)} %all-to-all-done.2.red1) | copy-start | bytes 98308
  92.5 38.8 %copy-start.4 = (f32[16,4,768]{2,1,0:T(4,128)}, f32[16,4,768]{2,1,0:T(4,128)S(1)}, u32[]{:S(2)}) copy-start(f32[16,4,768]{2,1,0:T(4,128)S(1)} %get-tuple-element.13.v1) | copy-start | bytes 589828
  92.5 27.1 %all-to-all-start.4 = ((f32[8,8,128]{2,1,0:T(8,128)}), f32[8,8,128]{2,1,0:T(8,128)S(1)}, u32[]{:S(2)}, u32[]{:S(2)}) async-start(f32[8,8,128]{2,1,0:T(8,128)} %get-tuple-element.12), calls=%async_computation.4 | async-start | bytes 65536 | tf_op jit(solution)/shard_map/all_to_all | solution.py:415
  98.6 25.3 %copy-start.11 = (f32[2,3,544]{2,0,1:T(2,128)S(1)}, f32[2,3,544]{2,0,1:T(2,128)}, u32[]{:S(2)}) copy-start(f32[2,3,544]{2,0,1:T(2,128)} %param.8) | copy-start | bytes 39172
  98.7 25.3 %copy-start.12 = (f32[2,544]{1,0:T(2,128)S(1)}, f32[2,544]{1,0:T(2,128)}, u32[]{:S(2)}) copy-start(f32[2,544]{1,0:T(2,128)} %param.9) | copy-start | bytes 13060
  119.6 49.5 %copy-start.2 = (f32[8,8,128]{2,1,0:T(8,128)}, f32[8,8,128]{2,1,0:T(8,128)S(1)}, u32[]{:S(2)}) copy-start(f32[8,8,128]{2,1,0:T(8,128)S(1)} %all-to-all-done.4.red2) | copy-start | bytes 98308
  120.4 10.9 %all-to-all-start.5 = ((f32[16,4,768]{2,1,0:T(4,128)}), f32[16,4,768]{2,1,0:T(4,128)S(1)}, u32[]{:S(2)}, u32[]{:S(2)}) async-start(f32[16,4,768]{2,1,0:T(4,128)} %post2.1.s2), calls=%async_computation.5 | async-start | bytes 393216 | tf_op jit(solution)/shard_map/all_to_all | solution.py:415
  132.4 0.7 copy-start.7
  133.1 10.5 %all-to-all-start.6 = ((f32[8,8,128]{2,1,0:T(8,128)}), f32[8,8,128]{2,1,0:T(8,128)S(1)}, u32[]{:S(2)}, u32[]{:S(2)}) async-start(f32[8,8,128]{2,1,0:T(8,128)} %get-tuple-element.14), calls=%async_computation.6 | async-start | bytes 65536 | tf_op jit(solution)/shard_map/all_to_all | solution.py:415
  144.5 26.7 %all-to-all-start.8 = ((f32[16,2,8,640]{3,2,1,0:T(8,128)}), f32[16,2,8,640]{3,2,1,0:T(8,128)S(1)}, u32[]{:S(2)}, u32[]{:S(2)}) async-start(f32[16,2,8,640]{3,2,1,0:T(8,128)} %broadcast_in_dim.28), calls=%async_computation.8 | async-start | bytes 1310720 | tf_op jit(solution)/shard_map/all_to_all | solution.py:415
  170.3 0.8 copy-start.6
  171.2 23.9 %copy-start.1 = (f32[8,8,128]{2,1,0:T(8,128)S(1)}, f32[8,8,128]{2,1,0:T(8,128)}, u32[]{:S(2)}) copy-start(f32[8,8,128]{2,1,0:T(8,128)} %copy-done) | copy-start | bytes 98308
  171.2 23.9 %copy-start.3 = (f32[8,8,128]{2,1,0:T(8,128)S(1)}, f32[8,8,128]{2,1,0:T(8,128)}, u32[]{:S(2)}) copy-start(f32[8,8,128]{2,1,0:T(8,128)} %copy-done.2) | copy-start | bytes 98308
  171.2 24.0 %copy-start.5 = (f32[16,4,768]{2,1,0:T(4,128)S(1)}, f32[16,4,768]{2,1,0:T(4,128)}, u32[]{:S(2)}) copy-start(f32[16,4,768]{2,1,0:T(4,128)} %copy-done.4) | copy-start | bytes 589828
  171.2 52.3 %all-to-all-start.7 = ((f32[128,8,128]{2,1,0:T(8,128)}), f32[128,8,128]{2,1,0:T(8,128)S(1)}, u32[]{:S(2)}, u32[]{:S(2)}) async-start(f32[128,8,128]{2,1,0:T(8,128)} %copy-done.6), calls=%async_computation.7 | async-start | bytes 1048576 | tf_op jit(solution)/shard_map/all_to_all | solution.py:415
  179.2 0.7 copy-start.9
  195.1 0.9 copy-start.8

commit v2 on v0

v2 whole, which is shorter than its diff:
```python
import math

import jax
import jax.numpy as jnp
from jax import lax
from jax.experimental import pallas as pl
from jax.experimental.pallas import tpu as pltpu
from jax.sharding import PartitionSpec as P

F32 = jnp.float32
BF16 = jnp.bfloat16
AXES = ("wall", "cell")
E2 = 0.1 * 0.1
FLOOR = 1e-06
SCALE = 1.0 / (8.0 * math.pi)
VMEM_LIMIT = 40 * 2**20


def row_of(n):
    return lax.broadcasted_iota(jnp.int32, (8, n), 0)


def split3(a):
    high = a.astype(BF16).astype(F32)
    rest = a - high
    mid = rest.astype(BF16).astype(F32)
    low = (rest - mid).astype(BF16).astype(F32)
    return high, mid, low


def target_factor(points):
    row = row_of(points.shape[1])
    coords = jnp.where(row < 3, points, 0.0)
    norm2 = jnp.sum(coords * coords, axis=0, keepdims=True) + E2
    eight = jnp.where(row < 3, -2.0 * coords, jnp.where(row == 3, 1.0, jnp.where(row == 4, norm2, 0.0)))
    h, m, l = split3(eight)
    return jnp.concatenate([h, m, l, h, m, h], axis=0)


def source_factor(points):
    row = row_of(points.shape[1])
    coords = jnp.where(row < 3, points, 0.0)
    norm2 = jnp.sum(coords * coords, axis=0, keepdims=True)
    eight = jnp.where(row < 3, coords, jnp.where(row == 3, norm2, jnp.where(row == 4, 1.0, 0.0)))
    h, m, l = split3(eight)
    return jnp.concatenate([h, h, h, m, m, l], axis=0)


def upright(a):
    wide = jnp.concatenate([a, jnp.zeros((128 - a.shape[0], a.shape[1]), F32)], axis=0)
    return jnp.transpose(wide)[:, : a.shape[0]].astype(BF16)


def moment_rows(points, twice):
    row = row_of(points.shape[1])
    coords = jnp.where(row < 3, points, 0.0)
    y0, y1, y2 = points[0:1], points[1:2], points[2:3]
    norm2 = jnp.sum(coords * coords, axis=0, keepdims=True)
    inner = jnp.sum(coords * twice, axis=0, keepdims=True)
    e = norm2 * twice + inner * coords
    first = twice * jnp.where(row < 4, 1.0, y0)
    first = jnp.where(row == 3, e[0:1], jnp.where(row == 7, e[1:2], first))
    second = twice * jnp.where(row < 4, y1, y2)
    second = jnp.where(row == 3, e[2:3], second)
    return [first, second]


def moment_block(groups):
    parts = [split3(g) for g in groups]
    return jnp.concatenate([p[k] for k in range(3) for p in parts], axis=0).astype(BF16)


def kernel_values(shifted, hilo):
    inv = lax.rsqrt(shifted)
    kern = inv * inv * inv
    high = kern.astype(BF16)
    return [high, (kern - high.astype(F32)).astype(BF16)] if hilo else [high]


def add_chunk(acc, sources, targets, moments, hilo):
    parts = kernel_values(jnp.dot(sources, targets, preferred_element_type=F32), hilo)
    acc[...] += jnp.dot(moments, parts[0], preferred_element_type=F32)
    if hilo:
        acc[0:32, :] += jnp.dot(moments[0:32], parts[1], preferred_element_type=F32)
    return parts[0]


def assemble(points, rows):
    f, t0, t1, t2 = rows[0:4], rows[4:8], rows[8:12], rows[12:16]
    n = points.shape[1]
    row = lax.broadcasted_iota(jnp.int32, (4, n), 0)
    x4 = jnp.where(row < 3, points[0:4], 0.0)
    x0, x1, x2 = x4[0:1], x4[1:2], x4[2:3]
    norm2 = jnp.sum(x4 * x4, axis=0, keepdims=True)
    along = jnp.sum(x4 * f, axis=0, keepdims=True) - (t0[0:1] + t1[1:2] + t2[2:3])
    s0 = jnp.sum(x4 * t0, axis=0, keepdims=True)
    s1 = jnp.sum(x4 * t1, axis=0, keepdims=True)
    s2 = jnp.sum(x4 * t2, axis=0, keepdims=True)
    e = jnp.where(row == 0, f[3:4] - s0, jnp.where(row == 1, t0[3:4] - s1, t1[3:4] - s2))
    return jnp.where(row < 3, (norm2 + 2.0 * E2) * f + e - 2.0 * (x0 * t0 + x1 * t1 + x2 * t2) + x4 * along, 0.0)


def velocity(points, acc):
    return assemble(points, acc[0:16] + acc[16:32] + acc[32:48])


def solve_small(hess, beta, size):
    zero = jnp.zeros_like(beta)
    upper = [[hess.get((r, c), zero) for c in range(size)] for r in range(size + 1)]
    targets = [beta] + [zero] * size
    cosines, sines = [], []
    for column in range(size):
        for prior in range(column):
            a, b = upper[prior][column], upper[prior + 1][column]
            upper[prior][column] = cosines[prior] * a + sines[prior] * b
            upper[prior + 1][column] = cosines[prior] * b - sines[prior] * a
        a, b = upper[column][column], upper[column + 1][column]
        radius = jnp.sqrt(a * a + b * b)
        cosines.append(a / radius)
        sines.append(b / radius)
        upper[column][column] = radius
        targets[column + 1] = -sines[column] * targets[column]
        targets[column] = cosines[column] * targets[column]
    weights = [None] * size
    for column in reversed(range(size)):
        part = targets[column]
        for later in range(column + 1, size):
            part = part - upper[column][later] * weights[later]
        weights[column] = part / upper[column][column]
    return weights


def row_with(values, start):
    lane = lax.broadcasted_iota(jnp.int32, (1, 128), 1)
    row = jnp.zeros((1, 128), F32)
    for k, v in enumerate(values):
        row = jnp.where(lane == start + k, jnp.broadcast_to(v, (1, 128)), row)
    return row


def total(a):
    while a.ndim > 2:
        a = jnp.sum(a, axis=0)
    return jnp.sum(jnp.sum(a, axis=0, keepdims=True), axis=1, keepdims=True)


def call(body, outs, ins, name, scratch=(), smem=(), apart=(), apart_out=()):
    def whole(dims):
        return pl.BlockSpec(dims, lambda i: (0,) * len(dims))

    in_specs = []
    for k, x in enumerate(ins):
        if k in smem:
            in_specs.append(pl.BlockSpec(memory_space=pltpu.SMEM))
        elif k in apart:
            in_specs.append(pl.BlockSpec(memory_space=pltpu.HBM))
        else:
            in_specs.append(whole(x.shape))
    out_specs = [
        pl.BlockSpec(memory_space=pltpu.HBM) if k in apart_out else whole(x.shape) for k, x in enumerate(outs)
    ]
    return pl.pallas_call(
        body,
        grid=(1,),
        out_shape=outs,
        in_specs=in_specs,
        out_specs=out_specs,
        scratch_shapes=list(scratch),
        compiler_params=pltpu.CompilerParams(vmem_limit_bytes=VMEM_LIMIT),
        name=name,
    )(*ins)


def shape(*dims, dtype=F32):
    return jax.ShapeDtypeStruct(dims, dtype)


def pack_body(centre, *refs):
    count = 6
    given, (mine, own, sent_wall, sent_cells) = refs[:count], refs[count : count + 4]
    held, sems = refs[count + 4 : 2 * count + 4], refs[2 * count + 4]
    moves = [pltpu.make_async_copy(x, y, sems.at[k]) for k, (x, y) in enumerate(zip(given, held))]
    for m in moves:
        m.start()
    for m in moves:
        m.wait()
    points, area, data, cell_points, cell_force, cell_weight = held
    n = points.shape[1]
    row = lax.broadcasted_iota(jnp.int32, (3, n), 0)
    mine[0:3] = points[...] - jnp.where(row == 0, centre[0], 0.0)
    mine[3:4] = area[...]
    mine[4:7] = data[...]
    mine[7:8] = jnp.zeros((1, n), F32)
    used = cell_points.shape[2]
    own[...] = jnp.zeros_like(own)
    for i in range(own.shape[0]):
        own[i, 0:3, 0:used] = cell_points[:, i, :]
        own[i, 4:7, 0:used] = cell_force[:, i, :] * cell_weight[i : i + 1, :]
    for p in range(sent_wall.shape[0]):
        sent_wall[p] = mine[...]
        sent_cells[p] = own[...]


def near_body(first, partners, own, everyone, out, sources, acc):
    cells = own.shape[0]
    width = own.shape[2]
    used = out.shape[2]
    row = row_of(width)
    r = row_of(THREE * width)
    for i in range(cells):
        mine = own[i]
        centre = jnp.where(row < 3, mine[:, 0:1], 0.0)
        for k in range(THREE):
            slot = first + k
            if slot == 0:
                sources[:, 0:width] = mine - centre
                continue
            n = partners[i, slot - 1]
            there = jnp.maximum(n, 0)
            other = everyone[there // cells, there % cells] - centre
            keep = jnp.where(n >= 0, 1.0, 0.0)
            sources[:, k * width : (k + 1) * width] = jnp.where(row >= 4, other * keep, other)
        targets = target_factor(mine - centre).astype(BF16)[:, :used]
        pts = sources[...]
        twice = SCALE * jnp.where(r >= 4, pts, pltpu.roll(pts, 4, 0))
        acc[...] = jnp.zeros_like(acc)
        add_chunk(acc, upright(source_factor(pts)), targets, moment_block(moment_rows(pts, twice)), True)
        out[i] = velocity((mine - centre)[:, :used], acc[...])


def parcels(near, far, sems, inward):
    n = near.shape[0] // PARCELS
    moves = []
    for k in range(PARCELS):
        here, there = near.at[pl.ds(k * n, n)], far.at[pl.ds(k * n, n)]
        moves.append(pltpu.make_async_copy(*((there, here) if inward else (here, there)), sems.at[k]))
    return n, moves


def first_body(mine, group, store, out, state, kept, acc, sems):
    targets = target_factor(mine[...]).astype(BF16)
    row = row_of(mine.shape[1])
    norm2 = total(jnp.where(row >= 4, group[...] * group[...], 0.0))
    size = jnp.sqrt(norm2 + TINY)
    state[...] = row_with([size, norm2 / (size * size)], 0)
    acc[...] = jnp.zeros_like(acc)

    def step(c, _):
        pts = group[c]
        twice = (SCALE * pts[3:4] / size) * jnp.where(row >= 4, pts, pltpu.roll(pts, 4, 0))
        moments = moment_block(moment_rows(pts, twice))
        kept[c] = add_chunk(acc, upright(source_factor(pts)), targets, moments, HILO_FIRST)
        return 0

    n, moves = parcels(kept, store, sems, False)
    for k, move in enumerate(moves):
        lax.fori_loop(k * n, (k + 1) * n, step, 0)
        move.start()
    vel = velocity(mine[...], acc[...])
    for p in range(out.shape[0]):
        out[p] = vel
    for move in moves:
        move.wait()


def fetch(store, kept, sems):
    n, moves = parcels(kept, store, sems, True)
    for move in moves:
        move.start()


def next_vector(group, state0, earlier, image, vector):
    basis = [data_rows(group[...]) / state0[0:1, 0:1]] + [q[...] for q in earlier]
    s = image[...]
    inner = [total(s * q) for q in basis]
    for b, q in zip(inner, basis):
        s = s - b * q
    norm2 = total(s * s)
    size = jnp.sqrt(norm2 + TINY)
    vector[...] = s / size
    return inner + [size, norm2 / (size * size)]


def apply_vector(mine, group, store, vector, kept, acc, sems):
    acc[...] = jnp.zeros_like(acc)

    def step(c, _):
        pts = group[c]
        four = vector[c] * (SCALE * pts[3:4])
        moments = moment_block(moment_rows(pts, jnp.concatenate([four, four], axis=0)))
        acc[...] += jnp.dot(moments, kept[c], preferred_element_type=F32)
        return 0

    n, moves = parcels(kept, store, sems, True)
    for k, move in enumerate(moves):
        move.wait()
        lax.fori_loop(k * n, (k + 1) * n, step, 0)
    return velocity(mine[...], acc[...])


def second_body(mine, group, store, state0, image, after, vector, out, state, kept, acc, sems):
    fetch(store, kept, sems)
    state[...] = row_with(next_vector(group, state0, [], image, vector), 2)
    vel = apply_vector(mine, group, store, vector, kept, acc, sems)
    for p in range(out.shape[0]):
        out[p] = vel


def third_body(mine, group, store, state0, q1, image, after, vector, out, state, kept, acc, sems):
    fetch(store, kept, sems)
    state[...] = row_with(next_vector(group, state0, [q1], image, vector), 5)
    vel = apply_vector(mine, group, store, vector, kept, acc, sems)
    for p in range(out.shape[0]):
        out[p] = vel


def fourth_body(at, mine, group, store, state0, state1, state2, q1, q2, image, after, vector, basis, out, kept, acc, sems):
    fetch(store, kept, sems)
    state3 = row_with(next_vector(group, state0, [q1, q2], image, vector), 9)
    vel = apply_vector(mine, group, store, vector, kept, acc, sems)
    own = [mine[4:8] / state0[0:1, 0:1]] + [q[at[0]] for q in (q1, q2, vector)]
    for k, q in enumerate(own):
        basis[k] = q
    last = row_with([total(vel * q) for q in own] + [total(vel * vel)], 14)
    out[...] = jnp.broadcast_to(state0[...] + state1[...] + state2[...] + state3 + last, out.shape)


def data_rows(block):
    return block[:, 4:8, :]


def cells_body(centre, state0, own, group, q1, q2, q3, out, left, acc):
    used = out.shape[3]
    width = own.shape[2]
    shift = jnp.where(row_of(width) == 0, centre[0], 0.0)
    size = state0[0:1, 0:1]
    cells = own.shape[0]
    for i in range(cells):
        left[i * used : (i + 1) * used, :] = upright(target_factor(own[i] - shift))[:used]
    acc[...] = jnp.zeros_like(acc)

    def step(c, _):
        pts = group[c]
        area = SCALE * pts[3:4]
        groups = []
        for v in (pts[4:8] / size, q1[c], q2[c], q3[c]):
            four = area * v
            groups += moment_rows(pts, jnp.concatenate([four, four], axis=0))
        moments = moment_block(groups)
        shifted = jnp.dot(left[...], source_factor(pts).astype(BF16), preferred_element_type=F32)
        for part in kernel_values(shifted, HILO_CELLS):
            acc[...] += lax.dot_general(part, moments, (((1,), (1,)), ((), ())), preferred_element_type=F32)
        return 0

    lax.fori_loop(0, group.shape[0], step, 0)
    for i in range(cells):
        part = acc[i * used : (i + 1) * used, :]
        full = jnp.concatenate([part, jnp.zeros((width - used, part.shape[1]), F32)], axis=0)
        full = jnp.concatenate([full, jnp.zeros((width, 256 - part.shape[1]), F32)], axis=1)
        rows = jnp.transpose(full)
        for k in range(4):
            sums = rows[16 * k : 16 * k + 16] + rows[64 + 16 * k : 80 + 16 * k] + rows[128 + 16 * k : 144 + 16 * k]
            out[k, i] = assemble(own[i] - shift, sums)[:, :used]


def krylov(local, gram, start, size):
    def dot(a, b):
        return sum(jnp.sum(gram[k] * x * y, axis=0, keepdims=True) for k, (x, y) in enumerate(zip(a, b)))

    beta = jnp.sqrt(dot([start], [start]) + FLOOR)
    basis = [[start / beta]]
    hess = {}
    for j in range(size):
        v = basis[j]
        w = []
        for k in range(j + 2):
            part = sum(local[(k, m)] * v[m] for m in range(max(k - 1, 0), j + 1))
            w.append(0.5 * v[k] + part if k <= j else part)
        for i in range(j + 1):
            h = dot(w, basis[i])
            hess[(i, j)] = h
            w = [x - h * basis[i][k] if k <= i else x for k, x in enumerate(w)]
        h = jnp.sqrt(dot(w, w) + FLOOR)
        hess[(j + 1, j)] = h
        basis.append([x / h for x in w])
    y = solve_small(hess, beta, size)
    return [sum(y[j] * basis[j][k] for j in range(k, size)) for k in range(size)]


def last_body(at, red, basis, near0, near1, near2, wall, velocity_out, density_out):
    segments = 8
    peers = red.shape[0] // segments
    rows = [jnp.sum(red[s * peers : (s + 1) * peers, :], axis=0, keepdims=True) for s in range(segments)]
    table = jnp.concatenate(rows, axis=0)
    same = lambda k: table[:, k : k + 1] * (1.0 / peers)
    local, gram = {}, [same(1)]
    start = same(0)
    for m, first in ((0, 2), (1, 5), (2, 9)):
        for k in range(m + 2):
            local[(k, m)] = same(first + k)
        gram.append(same(first + m + 2))
    norm2 = table[:, 18:19]
    for k in range(4):
        inner = table[:, 14 + k : 15 + k]
        local[(k, 3)] = inner
        norm2 = norm2 - inner * inner * (2.0 - gram[k])
    norm2 = jnp.maximum(norm2, 0.0)
    size = jnp.sqrt(norm2 + TINY)
    local[(4, 3)] = size
    gram.append(norm2 / (size * size))
    coords = krylov(local, gram, start, 4)
    mine = lax.broadcasted_iota(jnp.int32, (segments, 1), 0) == at[0]
    z = [jnp.sum(jnp.where(mine, x, 0.0), axis=0, keepdims=True) for x in coords]
    density = z[0] * basis[0]
    for k in range(1, 4):
        density = density + z[k] * basis[k]
    density_out[...] = density[0:3]
    for i in range(near0.shape[0]):
        part = near0[i] + near1[i] + near2[i]
        for k in range(4):
            part = part + z[k] * wall[k, i]
        velocity_out[:, i, :] = part[0:3]


HILO_FIRST = True
HILO = False
HILO_CELLS = False
TINY = 1e-30
THREE = 3
PARCELS = 4


def swap(x, axes):
    return lax.all_to_all(x, axes, 0, 0, tiled=True)


def per_device(cell_points, cell_force, cell_weight, partners, wall_points, wall_area, wall_data):
    cells, _, surface = cell_points.shape
    points = wall_points.shape[1]
    segments, peers = lax.axis_size("wall"), lax.axis_size("cell")
    width = -(-surface // 128) * 128
    segment = lax.axis_index("wall")
    centre = 8.0 * segment.astype(F32) + 4.0
    at = lax.axis_index("cell").astype(jnp.int32)[None]

    copies = shape(peers, 4, points)
    row = shape(1, 128)
    given = (
        wall_points,
        wall_area[None],
        wall_data,
        jnp.transpose(cell_points, (1, 0, 2)),
        jnp.transpose(cell_force, (1, 0, 2)),
        cell_weight,
    )
    mine, own, sent_wall, sent_cells = call(
        pack_body,
        [shape(8, points), shape(cells, 8, width), shape(peers, 8, points), shape(peers, cells, 8, width)],
        (centre[None], *given),
        "pack",
        [pltpu.VMEM(x.shape, F32) for x in given] + [pltpu.SemaphoreType.DMA((len(given),))],
        smem=(0,),
        apart=range(1, 1 + len(given)),
    )
    group = swap(sent_wall, "cell")
    everyone = swap(sent_cells, "cell")
    scratch = (
        pltpu.VMEM((peers, points, points), BF16),
        pltpu.VMEM((48, points), F32),
        pltpu.SemaphoreType.DMA((PARCELS,)),
    )

    def near(k):
        return call(
            lambda *refs: near_body(THREE * k, *refs),
            [shape(cells, 4, surface)],
            (partners, own, everyone),
            "near" + str(k),
            (pltpu.VMEM((8, THREE * width), F32), pltpu.VMEM((48, surface), F32)),
            smem=(0,),
        )[0]

    store, s0, state0 = call(
        first_body,
        [shape(peers, points, points, dtype=BF16), copies, row],
        (mine, group),
        "first",
        scratch,
        apart_out=(0,),
    )
    near0 = near(0)
    q1, s1, state1 = call(
        second_body,
        [copies, copies, row],
        (mine, group, store, state0, swap(s0, "cell"), near0),
        "second",
        scratch,
        apart=(2, 5),
    )
    near1 = near(1)
    q2, s2, state2 = call(
        third_body,
        [copies, copies, row],
        (mine, group, store, state0, q1, swap(s1, "cell"), near1),
        "third",
        scratch,
        apart=(2, 6),
    )
    near2 = near(2)
    q3, basis, sums = call(
        fourth_body,
        [copies, shape(4, 4, points), shape(segments * peers, 128)],
        (at, mine, group, store, state0, state1, state2, q1, q2, swap(s2, "cell"), near2),
        "fourth",
        scratch,
        smem=(0,),
        apart=(3, 10),
    )
    red = swap(sums, AXES)
    (wall,) = call(
        cells_body,
        [shape(4, cells, 4, surface)],
        (centre[None], state0, own, group, q1, q2, q3),
        "cells",
        (pltpu.VMEM((cells * surface, 48), BF16), pltpu.VMEM((cells * surface, 192), F32)),
        smem=(0,),
    )
    velocity_out, density = call(
        last_body,
        [shape(3, cells, surface), shape(3, points)],
        (segment.astype(jnp.int32)[None], red, basis, near0, near1, near2, wall),
        "last",
        smem=(0,),
    )
    return jnp.transpose(velocity_out, (1, 0, 2)), density


def solution(mesh):
    in_specs = (
        P(AXES, None, None),
        P(AXES, None, None),
        P(AXES, None),
        P(AXES, None),
        P(None, AXES),
        P(AXES),
        P(None, AXES),
    )
    out_specs = (P(AXES, None, None), P(None, AXES))
    step = jax.shard_map(per_device, mesh=mesh, in_specs=in_specs, out_specs=out_specs, check_vma=False)
    return step
```

time: 906 us -> 141 us (0.16); the launches traced: 894 us -> 140 us
  other arithmetic: 517 us -> 0 us
  blocking collectives: 302 us -> 16.5 us
  Pallas kernels: 0 us -> 80.2 us
  between operations: 18.6 us -> 0.78 us
  waiting for transfers between devices: 21.7 us -> 7.24 us
  starting transfers between devices: 18.6 us -> 30.6 us
    reduce_sum x237 -> x0, other arithmetic: 415 us -> none  [the longest x114 226 us: stokeslet(): return jnp.sum(factor[None] * terms, axis=2)]
    psum x36 -> x0, blocking collectives: 285 us -> none  [one_axis_at_a_time(): x = lax.psum(x, axis)]
    div x114 -> x0, other arithmetic: 90 us -> none  [stokeslet(): factor = 1.0 / (8.0 * math.pi * shifted * jnp.sqrt(shifted))]
    pallas_call x0 -> x10, Pallas kernels: none -> 80.2 us  [call(): pl.pallas_call(body, grid=(1,), out_shape=outs, in_specs=in_specs, out_sp...]
    all_gather x1 -> x0, blocking collectives: 17.4 us -> none  [sent_together_2(): out = lax.all_gather(both, axis, axis=dim, tiled=True)]
    all_to_all x0 -> x1, blocking collectives: none -> 16.5 us  [swap(): return lax.all_to_all(x, axes, 0, 0, tiled=True)]
    all_to_all x5, waiting for transfers between devices: 21.7 us -> 7.24 us  [swap(): return lax.all_to_all(x, axes, 0, 0, tiled=True)]
    all_to_all x5, starting transfers between devices: 18.6 us -> 30.6 us  [swap(): return lax.all_to_all(x, axes, 0, 0, tiled=True)]
  transfers between devices with their start and end apart: 5 -> 5, of which waited for: 3 -> 3; matrix products, arithmetic and copies ran while one was open for 15% -> 0% of each run, Pallas kernels for 0% -> 35%
where the time goes in v2:
time: 141 us; the launch traced here: 140 us
  Pallas kernels  80.2 us (57%)
  starting transfers between devices  30.6 us (22%)
  blocking collectives  16.5 us (12%)
  waiting for transfers between devices  7.24 us (5%)
  local copies, waits for them, and re-layouts  4.9 us (3%)
    pallas_call x10, Pallas kernels, call(): pl.pallas_call(body, grid=(1,), out_shape=outs, in_specs=in_specs, out_sp...  80.2 us
    all_to_all x5, starting transfers between devices, swap(): return lax.all_to_all(x, axes, 0, 0, tiled=True)  30.6 us
    all_to_all x1, blocking collectives, swap(): return lax.all_to_all(x, axes, 0, 0, tiled=True)  16.5 us
    all_to_all x5, waiting for transfers between devices, swap(): return lax.all_to_all(x, axes, 0, 0, tiled=True)  7.24 us
    unnamed x14, local copies, waits for them, and re-layouts  4.21 us
  transfers between devices with their start and end apart: 5, of which 3 were waited for; matrix products, arithmetic and copies ran while one was open for 0% of the time, Pallas kernels for 35%

profile of v2, /device:TPU:1, one launch (start us, length us, event | category | flops | bytes accessed | tf_op | source)
XLA Modules:
  0.0 140.2 jit_solution(18363910337409797322)
XLA Ops:
  0.6 0.0 copy-start.5
  0.6 0.7 broadcast_in_dim.16.refs_1_
  1.3 0.0 copy-start
  1.3 0.7 copy-done
  2.1 0.0 copy-start.1
  2.1 0.7 copy-done.1
  2.8 0.0 copy-start.2
  2.8 0.7 copy-done.2
  3.5 0.0 copy-start.3
  3.5 0.7 copy-done.3
  4.2 0.0 copy-start.6
  4.2 0.7 copy-done.6
  4.9 1.1 pack.1
  5.9 16.5 %all_to_all.36.group = f32[16,8,768]{2,1,0:T(8,128)S(1)} all-to-all(f32[16,8,768]{2,1,0:T(8,128)S(1)} %get-tuple-element.21), channel_id=1, replica_groups=mesh['wall'=8,'cell'=16] {'cell'}, dimensions={0} | all-to-all | bytes 786432 | tf_op jit(solution)/shard_map/all_to_all | solution.py:434
  22.4 4.1 %all-to-all-start.2 = ((f32[16,2,8,640]{3,2,1,0:T(8,128)}), f32[16,2,8,640]{3,2,1,0:T(8,128)S(1)}, u32[]{:S(2)}, u32[]{:S(2)}) async-start(f32[16,2,8,640]{3,2,1,0:T(8,128)} %get-tuple-element.26), calls=%async_computation.2 | async-start | bytes 1310720 | tf_op jit(solution)/shard_map/all_to_all | solution.py:434
  26.6 18.2 %first.1 = (bf16[16,768,768]{2,1,0:T(8,128)(2,1)}, f32[16,4,768]{2,1,0:T(4,128)}, f32[1,128]{1,0:T(1,128)S(1)}) custom-call(f32[8,768]{1,0:T(8,128)S(1)} %get-tuple-element.20.mine, f32[16,8,768]{2,1,0:T(8,128)S(1)} %all_to_all.36.group), custom_call_target="tpu_custom_call" | custom-call | tf_op jit(solution)/shard_map/first/pallas_call | solution.py:162
  44.8 0.0 all-to-all-done.2.refs_2_
  44.8 6.7 %all-to-all-start.1 = ((f32[16,4,768]{2,1,0:T(4,128)}), f32[16,4,768]{2,1,0:T(4,128)S(1)}, u32[]{:S(2)}, u32[]{:S(2)}) async-start(f32[16,4,768]{2,1,0:T(4,128)} %get-tuple-element.24), calls=%async_computation.1 | async-start | bytes 393216 | tf_op jit(solution)/shard_map/all_to_all | solution.py:434
  51.5 0.0 copy-start.4
  51.5 0.7 copy-done.4
  52.2 4.3 %near0.1.after = f32[2,4,544]{2,1,0:T(4,128)S(1)} custom-call(s32[2,8]{1,0:T(2,128)S(1)} %copy-done.4, f32[2,8,640]{2,1,0:T(8,128)S(1)} %get-tuple-element.25.refs_1_.own, f32[16,2,8,640]{3,2,1,0:T(8,128)S(1)} %all-to-all-done.2.refs_2_), custom_call_target="tpu_custom_call" | custom-call | tf_op jit(solution)/shard_map/near0/pallas_call | solution.py:162
  56.5 2.0 %all-to-all-done.1.image = f32[16,4,768]{2,1,0:T(4,128)S(1)} async-done(((f32[16,4,768]{2,1,0:T(4,128)}), f32[16,4,768]{2,1,0:T(4,128)S(1)}, u32[]{:S(2)}, u32[]{:S(2)}) %all-to-all-start.1) | async-done | bytes 196640 | tf_op jit(solution)/shard_map/all_to_all | solution.py:434
  58.4 8.7 %second.1 = (f32[16,4,768]{2,1,0:T(4,128)S(1)}, f32[16,4,768]{2,1,0:T(4,128)}, f32[1,128]{1,0:T(1,128)S(1)}) custom-call(f32[8,768]{1,0:T(8,128)S(1)} %get-tuple-element.20.mine, f32[16,8,768]{2,1,0:T(8,128)S(1)} %all_to_all.36.group, bf16[16,768,768]{2,1,0:T(8,128)(2,1)} %get-tuple-element.22.store, f32[1,128]{1,0:T(1,128)S(1)} %get-tuple-element.23.state0, ...), custom_call_target="tpu_custom_call" | custom-call | tf_op jit(solution)/shard_map/second/pallas_call | solution.py:162
  67.1 4.7 %all-to-all-start.3 = ((f32[16,4,768]{2,1,0:T(4,128)}), f32[16,4,768]{2,1,0:T(4,128)S(1)}, u32[]{:S(2)}, u32[]{:S(2)}) async-start(f32[16,4,768]{2,1,0:T(4,128)} %get-tuple-element.29), calls=%async_computation.3 | async-start | bytes 393216 | tf_op jit(solution)/shard_map/all_to_all | solution.py:434
  71.8 0.0 copy-done.5
  71.8 4.3 %near1.1.after = f32[2,4,544]{2,1,0:T(4,128)S(1)} custom-call(s32[2,8]{1,0:T(2,128)S(1)} %copy-done.5, f32[2,8,640]{2,1,0:T(8,128)S(1)} %get-tuple-element.25.refs_1_.own, f32[16,2,8,640]{3,2,1,0:T(8,128)S(1)} %all-to-all-done.2.refs_2_), custom_call_target="tpu_custom_call" | custom-call | tf_op jit(solution)/shard_map/near1/pallas_call | solution.py:162
  76.1 2.6 %all-to-all-done.3.image = f32[16,4,768]{2,1,0:T(4,128)S(1)} async-done(((f32[16,4,768]{2,1,0:T(4,128)}), f32[16,4,768]{2,1,0:T(4,128)S(1)}, u32[]{:S(2)}, u32[]{:S(2)}) %all-to-all-start.3) | async-done | bytes 196640 | tf_op jit(solution)/shard_map/all_to_all | solution.py:434
  78.7 8.7 %third.1 = (f32[16,4,768]{2,1,0:T(4,128)S(1)}, f32[16,4,768]{2,1,0:T(4,128)}, f32[1,128]{1,0:T(1,128)S(1)}) custom-call(f32[8,768]{1,0:T(8,128)S(1)} %get-tuple-element.20.mine, f32[16,8,768]{2,1,0:T(8,128)S(1)} %all_to_all.36.group, bf16[16,768,768]{2,1,0:T(8,128)(2,1)} %get-tuple-element.22.store, f32[1,128]{1,0:T(1,128)S(1)} %get-tuple-element.23.state0, ...), custom_call_target="tpu_custom_call" | custom-call | tf_op jit(solution)/shard_map/third/pallas_call | solution.py:162
  87.4 4.0 %all-to-all-start.4 = ((f32[16,4,768]{2,1,0:T(4,128)}), f32[16,4,768]{2,1,0:T(4,128)S(1)}, u32[]{:S(2)}, u32[]{:S(2)}) async-start(f32[16,4,768]{2,1,0:T(4,128)} %get-tuple-element.32), calls=%async_computation.4 | async-start | bytes 393216 | tf_op jit(solution)/shard_map/all_to_all | solution.py:434
  91.5 4.3 %near2.1.after = f32[2,4,544]{2,1,0:T(4,128)S(1)} custom-call(s32[2,8]{1,0:T(2,128)S(1)} %copy-done.5, f32[2,8,640]{2,1,0:T(8,128)S(1)} %get-tuple-element.25.refs_1_.own, f32[16,2,8,640]{3,2,1,0:T(8,128)S(1)} %all-to-all-done.2.refs_2_), custom_call_target="tpu_custom_call" | custom-call | tf_op jit(solution)/shard_map/near2/pallas_call | solution.py:162
  95.8 2.6 %all-to-all-done.4.image = f32[16,4,768]{2,1,0:T(4,128)S(1)} async-done(((f32[16,4,768]{2,1,0:T(4,128)}), f32[16,4,768]{2,1,0:T(4,128)S(1)}, u32[]{:S(2)}, u32[]{:S(2)}) %all-to-all-start.4) | async-done | bytes 196640 | tf_op jit(solution)/shard_map/all_to_all | solution.py:434
  98.4 9.0 %fourth.1 = (f32[16,4,768]{2,1,0:T(4,128)S(1)}, f32[4,4,768]{2,1,0:T(4,128)S(1)}, f32[128,128]{1,0:T(8,128)}) custom-call(s32[1]{0:T(128)} %bitcast.1.at, f32[8,768]{1,0:T(8,128)S(1)} %get-tuple-element.20.mine, f32[16,8,768]{2,1,0:T(8,128)S(1)} %all_to_all.36.group, bf16[16,768,768]{2,1,0:T(8,128)(2,1)} %get-tuple-element.22.store, ...), custom_call_target="tpu_custom_call" | custom-call | tf_op jit(solution)/shard_map/fourth/pallas_call | solution.py:162
  107.4 11.0 %all-to-all-start.5 = ((f32[128,1,128]{2,1,0:T(1,128)}), f32[128,1,128]{2,1,0:T(1,128)S(1)}, u32[]{:S(2)}, u32[]{:S(2)}) async-start(f32[128,1,128]{2,1,0:T(1,128)} %bitcast.6), calls=%async_computation.5 | async-start | bytes 131072 | tf_op jit(solution)/shard_map/all_to_all | solution.py:434
  118.5 17.5 %cells.1.wall = f32[4,2,4,544]{3,2,1,0:T(4,128)S(1)} custom-call(f32[1]{0:T(128)} %bitcast.2.centre, f32[1,128]{1,0:T(1,128)S(1)} %get-tuple-element.23.state0, f32[2,8,640]{2,1,0:T(8,128)S(1)} %get-tuple-element.25.refs_1_.own, f32[16,8,768]{2,1,0:T(8,128)S(1)} %all_to_all.36.group, f32[16,4,768]{2,1,0:T(4,128)S(1)} %get-tuple-element.28.q1, ...), custom_call_target="tpu_custom_call" | custom-call | tf_op jit(solution)/shard_map/cells/pallas_call | solution.py:162
  136.0 0.0 all-to-all-done.5
  136.0 4.1 %last.1 = (f32[3,2,544]{2,1,0:T(2,128)}, f32[3,768]{1,0:T(4,128)}) custom-call(s32[1]{0:T(128)} %bitcast.at, f32[128,128]{1,0:T(8,128)S(1)} %bitcast.10, f32[4,4,768]{2,1,0:T(4,128)S(1)} %get-tuple-element.34.basis, f32[2,4,544]{2,1,0:T(4,128)S(1)} %near0.1.after, f32[2,4,544]{2,1,0:T(4,128)S(1)} %near1.1.after, f32[2,4,544]{2,1,0:T(4,128)S(1)} %near2.1.after, ...), custom_call_target="tpu_custom_call" | custom-call | tf_op jit(solution)/shard_map/last/pallas_call | solution.py:162
Async XLA Ops:
  0.6 71.2 %copy-start.5 = (s32[2,8]{1,0:T(2,128)S(1)}, s32[2,8]{1,0:T(2,128)}, u32[]{:S(2)}) copy-start(s32[2,8]{1,0:T(2,128)} %refs_0_.7) | copy-start | bytes 196
  1.3 0.7 copy-start
  2.1 0.7 copy-start.1
  2.8 0.7 copy-start.2
  3.5 0.7 copy-start.3
  4.2 0.7 copy-start.6
  22.4 22.4 %all-to-all-start.2 = ((f32[16,2,8,640]{3,2,1,0:T(8,128)}), f32[16,2,8,640]{3,2,1,0:T(8,128)S(1)}, u32[]{:S(2)}, u32[]{:S(2)}) async-start(f32[16,2,8,640]{3,2,1,0:T(8,128)} %get-tuple-element.26), calls=%async_computation.2 | async-start | bytes 1310720 | tf_op jit(solution)/shard_map/all_to_all | solution.py:434
  44.8 13.6 %all-to-all-start.1 = ((f32[16,4,768]{2,1,0:T(4,128)}), f32[16,4,768]{2,1,0:T(4,128)S(1)}, u32[]{:S(2)}, u32[]{:S(2)}) async-start(f32[16,4,768]{2,1,0:T(4,128)} %get-tuple-element.24), calls=%async_computation.1 | async-start | bytes 393216 | tf_op jit(solution)/shard_map/all_to_all | solution.py:434
  51.5 0.7 copy-start.4
  67.1 11.6 %all-to-all-start.3 = ((f32[16,4,768]{2,1,0:T(4,128)}), f32[16,4,768]{2,1,0:T(4,128)S(1)}, u32[]{:S(2)}, u32[]{:S(2)}) async-start(f32[16,4,768]{2,1,0:T(4,128)} %get-tuple-element.29), calls=%async_computation.3 | async-start | bytes 393216 | tf_op jit(solution)/shard_map/all_to_all | solution.py:434
  87.4 11.0 %all-to-all-start.4 = ((f32[16,4,768]{2,1,0:T(4,128)}), f32[16,4,768]{2,1,0:T(4,128)S(1)}, u32[]{:S(2)}, u32[]{:S(2)}) async-start(f32[16,4,768]{2,1,0:T(4,128)} %get-tuple-element.32), calls=%async_computation.4 | async-start | bytes 393216 | tf_op jit(solution)/shard_map/all_to_all | solution.py:434
  107.4 28.6 %all-to-all-start.5 = ((f32[128,1,128]{2,1,0:T(1,128)}), f32[128,1,128]{2,1,0:T(1,128)S(1)}, u32[]{:S(2)}, u32[]{:S(2)}) async-start(f32[128,1,128]{2,1,0:T(1,128)} %bitcast.6), calls=%async_computation.5 | async-start | bytes 131072 | tf_op jit(solution)/shard_map/all_to_all | solution.py:434

commit v3 on v2

--- a/solution.py
+++ b/solution.py
@@ -13,7 +13,7 @@
 E2 = 0.1 * 0.1
 FLOOR = 1e-06
 SCALE = 1.0 / (8.0 * math.pi)
-VMEM_LIMIT = 40 * 2**20
+VMEM_LIMIT = 48 * 2**20
 
 
 def row_of(n):
@@ -188,7 +188,7 @@
     n = points.shape[1]
     row = lax.broadcasted_iota(jnp.int32, (3, n), 0)
     mine[0:3] = points[...] - jnp.where(row == 0, centre[0], 0.0)
-    mine[3:4] = area[...]
+    mine[3:4] = jnp.concatenate([area[k : k + 1] for k in range(area.shape[0])], axis=1)
     mine[4:7] = data[...]
     mine[7:8] = jnp.zeros((1, n), F32)
     used = cell_points.shape[2]
@@ -228,13 +228,29 @@
         out[i] = velocity((mine - centre)[:, :used], acc[...])
 
 
-def parcels(near, far, sems, inward):
-    n = near.shape[0] // PARCELS
-    moves = []
-    for k in range(PARCELS):
-        here, there = near.at[pl.ds(k * n, n)], far.at[pl.ds(k * n, n)]
-        moves.append(pltpu.make_async_copy(*((there, here) if inward else (here, there)), sems.at[k]))
-    return n, moves
+def parcel(near, far, sems, k, inward):
+    here, there = near.at[pl.ds(k * PART, PART)], far.at[pl.ds(k * PART, PART)]
+    return pltpu.make_async_copy(*((there, here) if inward else (here, there)), sems.at[k])
+
+
+def through(count, step, before=None, after=None):
+    def part(k, _):
+        if before is not None:
+            before(k)
+        lax.fori_loop(k * PART, (k + 1) * PART, step, 0)
+        if after is not None:
+            after(k)
+        return 0
+
+    lax.fori_loop(0, count // PART, part, 0)
+
+
+def each(count, act):
+    def one(k, _):
+        act(k)
+        return 0
+
+    lax.fori_loop(0, count, one, 0)
 
 
 def first_body(mine, group, store, out, state, kept, acc, sems):
@@ -252,21 +268,15 @@
         kept[c] = add_chunk(acc, upright(source_factor(pts)), targets, moments, HILO_FIRST)
         return 0
 
-    n, moves = parcels(kept, store, sems, False)
-    for k, move in enumerate(moves):
-        lax.fori_loop(k * n, (k + 1) * n, step, 0)
-        move.start()
+    through(group.shape[0], step, after=lambda k: parcel(kept, store, sems, k, False).start())
     vel = velocity(mine[...], acc[...])
     for p in range(out.shape[0]):
         out[p] = vel
-    for move in moves:
-        move.wait()
+    each(group.shape[0] // PART, lambda k: parcel(kept, store, sems, k, False).wait())
 
 
 def fetch(store, kept, sems):
-    n, moves = parcels(kept, store, sems, True)
-    for move in moves:
-        move.start()
+    each(store.shape[0] // PART, lambda k: parcel(kept, store, sems, k, True).start())
 
 
 def next_vector(group, state0, earlier, image, vector):
@@ -281,43 +291,46 @@
     return inner + [size, norm2 / (size * size)]
 
 
-def apply_vector(mine, group, store, vector, kept, acc, sems):
+def apply_vector(mine, group, store, vector, kept, ready, acc, sems):
+    chunks = group.shape[0]
     acc[...] = jnp.zeros_like(acc)
 
-    def step(c, _):
+    def moments(c):
         pts = group[c]
         four = vector[c] * (SCALE * pts[3:4])
-        moments = moment_block(moment_rows(pts, jnp.concatenate([four, four], axis=0)))
-        acc[...] += jnp.dot(moments, kept[c], preferred_element_type=F32)
+        return moment_block(moment_rows(pts, jnp.concatenate([four, four], axis=0)))
+
+    def step(c, _):
+        now = ready[c % 2]
+        ready[(c + 1) % 2] = moments((c + 1) % chunks)
+        acc[...] += jnp.dot(now, kept[c], preferred_element_type=F32)
         return 0
 
-    n, moves = parcels(kept, store, sems, True)
-    for k, move in enumerate(moves):
-        move.wait()
-        lax.fori_loop(k * n, (k + 1) * n, step, 0)
+    ready[0] = moments(0)
+    through(chunks, step, before=lambda k: parcel(kept, store, sems, k, True).wait())
     return velocity(mine[...], acc[...])
 
 
-def second_body(mine, group, store, state0, image, after, vector, out, state, kept, acc, sems):
+def second_body(mine, group, store, state0, image, after, vector, out, state, kept, ready, acc, sems):
     fetch(store, kept, sems)
     state[...] = row_with(next_vector(group, state0, [], image, vector), 2)
-    vel = apply_vector(mine, group, store, vector, kept, acc, sems)
+    vel = apply_vector(mine, group, store, vector, kept, ready, acc, sems)
     for p in range(out.shape[0]):
         out[p] = vel
 
 
-def third_body(mine, group, store, state0, q1, image, after, vector, out, state, kept, acc, sems):
+def third_body(mine, group, store, state0, q1, image, after, vector, out, state, kept, ready, acc, sems):
     fetch(store, kept, sems)
     state[...] = row_with(next_vector(group, state0, [q1], image, vector), 5)
-    vel = apply_vector(mine, group, store, vector, kept, acc, sems)
+    vel = apply_vector(mine, group, store, vector, kept, ready, acc, sems)
     for p in range(out.shape[0]):
         out[p] = vel
 
 
-def fourth_body(at, mine, group, store, state0, state1, state2, q1, q2, image, after, vector, basis, out, kept, acc, sems):
+def fourth_body(at, mine, group, store, state0, state1, state2, q1, q2, image, after, vector, basis, out, kept, ready, acc, sems):
     fetch(store, kept, sems)
     state3 = row_with(next_vector(group, state0, [q1, q2], image, vector), 9)
-    vel = apply_vector(mine, group, store, vector, kept, acc, sems)
+    vel = apply_vector(mine, group, store, vector, kept, ready, acc, sems)
     own = [mine[4:8] / state0[0:1, 0:1]] + [q[at[0]] for q in (q1, q2, vector)]
     for k, q in enumerate(own):
         basis[k] = q
@@ -329,31 +342,36 @@
     return block[:, 4:8, :]
 
 
-def cells_body(centre, state0, own, group, q1, q2, q3, out, left, acc):
+def cells_body(centre, state0, own, group, q1, q2, q3, out, acc, left, ready):
     used = out.shape[3]
     width = own.shape[2]
     shift = jnp.where(row_of(width) == 0, centre[0], 0.0)
     size = state0[0:1, 0:1]
-    cells = own.shape[0]
-    for i in range(cells):
+    chunks = group.shape[0]
+    acc[...] = jnp.zeros_like(acc)
+    for i in range(own.shape[0]):
         left[i * used : (i + 1) * used, :] = upright(target_factor(own[i] - shift))[:used]
-    acc[...] = jnp.zeros_like(acc)
-
-    def step(c, _):
+
+    def moments(c):
         pts = group[c]
         area = SCALE * pts[3:4]
         groups = []
         for v in (pts[4:8] / size, q1[c], q2[c], q3[c]):
             four = area * v
             groups += moment_rows(pts, jnp.concatenate([four, four], axis=0))
-        moments = moment_block(groups)
-        shifted = jnp.dot(left[...], source_factor(pts).astype(BF16), preferred_element_type=F32)
-        for part in kernel_values(shifted, HILO_CELLS):
-            acc[...] += lax.dot_general(part, moments, (((1,), (1,)), ((), ())), preferred_element_type=F32)
+        return moment_block(groups)
+
+    def step(c, _):
+        now = ready[c % 2]
+        ready[(c + 1) % 2] = moments((c + 1) % chunks)
+        columns = source_factor(group[c]).astype(BF16)
+        values = kernel_values(jnp.dot(left[...], columns, preferred_element_type=F32), False)[0]
+        acc[...] += lax.dot_general(values, now, (((1,), (1,)), ((), ())), preferred_element_type=F32)
         return 0
 
-    lax.fori_loop(0, group.shape[0], step, 0)
-    for i in range(cells):
+    ready[0] = moments(0)
+    lax.fori_loop(0, chunks, step, 0)
+    for i in range(own.shape[0]):
         part = acc[i * used : (i + 1) * used, :]
         full = jnp.concatenate([part, jnp.zeros((width - used, part.shape[1]), F32)], axis=0)
         full = jnp.concatenate([full, jnp.zeros((width, 256 - part.shape[1]), F32)], axis=1)
@@ -365,7 +383,8 @@
 
 def krylov(local, gram, start, size):
     def dot(a, b):
-        return sum(jnp.sum(gram[k] * x * y, axis=0, keepdims=True) for k, (x, y) in enumerate(zip(a, b)))
+        both = sum(gram[k] * x * y for k, (x, y) in enumerate(zip(a, b)))
+        return jnp.broadcast_to(jnp.sum(both, axis=0, keepdims=True), both.shape)
 
     beta = jnp.sqrt(dot([start], [start]) + FLOOR)
     basis = [[start / beta]]
@@ -382,7 +401,8 @@
             w = [x - h * basis[i][k] if k <= i else x for k, x in enumerate(w)]
         h = jnp.sqrt(dot(w, w) + FLOOR)
         hess[(j + 1, j)] = h
-        basis.append([x / h for x in w])
+        inverse = 1.0 / h
+        basis.append([x * inverse for x in w])
     y = solve_small(hess, beta, size)
     return [sum(y[j] * basis[j][k] for j in range(k, size)) for k in range(size)]
 
@@ -392,16 +412,17 @@
     peers = red.shape[0] // segments
     rows = [jnp.sum(red[s * peers : (s + 1) * peers, :], axis=0, keepdims=True) for s in range(segments)]
     table = jnp.concatenate(rows, axis=0)
-    same = lambda k: table[:, k : k + 1] * (1.0 / peers)
+    column = lambda k: jnp.broadcast_to(table[:, k : k + 1], (segments, 128))
+    same = lambda k: column(k) * (1.0 / peers)
     local, gram = {}, [same(1)]
     start = same(0)
     for m, first in ((0, 2), (1, 5), (2, 9)):
         for k in range(m + 2):
             local[(k, m)] = same(first + k)
         gram.append(same(first + m + 2))
-    norm2 = table[:, 18:19]
+    norm2 = column(18)
     for k in range(4):
-        inner = table[:, 14 + k : 15 + k]
+        inner = column(14 + k)
         local[(k, 3)] = inner
         norm2 = norm2 - inner * inner * (2.0 - gram[k])
     norm2 = jnp.maximum(norm2, 0.0)
@@ -409,25 +430,26 @@
     local[(4, 3)] = size
     gram.append(norm2 / (size * size))
     coords = krylov(local, gram, start, 4)
-    mine = lax.broadcasted_iota(jnp.int32, (segments, 1), 0) == at[0]
+    mine = lax.broadcasted_iota(jnp.int32, (segments, 128), 0) == at[0]
     z = [jnp.sum(jnp.where(mine, x, 0.0), axis=0, keepdims=True) for x in coords]
-    density = z[0] * basis[0]
+    points = basis.shape[2]
+    wide = [jnp.concatenate([x] * (points // 128), axis=1) for x in z]
+    density = wide[0] * basis[0]
     for k in range(1, 4):
-        density = density + z[k] * basis[k]
+        density = density + wide[k] * basis[k]
     density_out[...] = density[0:3]
     for i in range(near0.shape[0]):
         part = near0[i] + near1[i] + near2[i]
         for k in range(4):
-            part = part + z[k] * wall[k, i]
+            part = part + wide[k][:, : part.shape[1]] * wall[k, i]
         velocity_out[:, i, :] = part[0:3]
 
 
-HILO_FIRST = True
+HILO_FIRST = False
 HILO = False
-HILO_CELLS = False
 TINY = 1e-30
 THREE = 3
-PARCELS = 4
+PART = 2
 
 
 def swap(x, axes):
@@ -447,7 +469,7 @@
     row = shape(1, 128)
     given = (
         wall_points,
-        wall_area[None],
+        wall_area.reshape(points // 128, 128),
         wall_data,
         jnp.transpose(cell_points, (1, 0, 2)),
         jnp.transpose(cell_force, (1, 0, 2)),
@@ -456,7 +478,7 @@
     mine, own, sent_wall, sent_cells = call(
         pack_body,
         [shape(8, points), shape(cells, 8, width), shape(peers, 8, points), shape(peers, cells, 8, width)],
-        (centre[None], *given),
+        (centre[None], *(pltpu.with_memory_space_constraint(x, pltpu.HBM) for x in given)),
         "pack",
         [pltpu.VMEM(x.shape, F32) for x in given] + [pltpu.SemaphoreType.DMA((len(given),))],
         smem=(0,),
@@ -467,8 +489,9 @@
     scratch = (
         pltpu.VMEM((peers, points, points), BF16),
         pltpu.VMEM((48, points), F32),
-        pltpu.SemaphoreType.DMA((PARCELS,)),
-    )
+        pltpu.SemaphoreType.DMA((peers // PART,)),
+    )
+    later = (scratch[0], pltpu.VMEM((2, 48, points), BF16), *scratch[1:])
 
     def near(k):
         return call(
@@ -494,7 +517,7 @@
         [copies, copies, row],
         (mine, group, store, state0, swap(s0, "cell"), near0),
         "second",
-        scratch,
+        later,
         apart=(2, 5),
     )
     near1 = near(1)
@@ -503,7 +526,7 @@
         [copies, copies, row],
         (mine, group, store, state0, q1, swap(s1, "cell"), near1),
         "third",
-        scratch,
+        later,
         apart=(2, 6),
     )
     near2 = near(2)
@@ -512,7 +535,7 @@
         [copies, shape(4, 4, points), shape(segments * peers, 128)],
         (at, mine, group, store, state0, state1, state2, q1, q2, swap(s2, "cell"), near2),
         "fourth",
-        scratch,
+        later,
         smem=(0,),
         apart=(3, 10),
     )
@@ -522,7 +545,11 @@
         [shape(4, cells, 4, surface)],
         (centre[None], state0, own, group, q1, q2, q3),
         "cells",
-        (pltpu.VMEM((cells * surface, 48), BF16), pltpu.VMEM((cells * surface, 192), F32)),
+        (
+            pltpu.VMEM((cells * surface, 192), F32),
+            pltpu.VMEM((cells * surface, 48), BF16),
+            pltpu.VMEM((2, 192, points), BF16),
+        ),
         smem=(0,),
     )
     velocity_out, density = call(

time: 141 us -> 127 us (0.901)
  Pallas kernels: 80.2 us -> 70.8 us
  local copies, waits for them, and re-layouts: 4.9 us -> 0.68 us
    pallas_call x10, Pallas kernels: 80.2 us -> 70.8 us  [call(): pl.pallas_call(body, grid=(1,), out_shape=outs, in_specs=in_specs, out_sp...]
    unnamed x14 -> x4, local copies, waits for them, and re-layouts: 4.21 us -> 0.68 us
where the time goes in v3:
time: 127 us
  Pallas kernels  70.8 us (56%)
  starting transfers between devices  30.6 us (24%)
  blocking collectives  16.5 us (13%)
  waiting for transfers between devices  7.24 us (6%)
    pallas_call x10, Pallas kernels, call(): pl.pallas_call(body, grid=(1,), out_shape=outs, in_specs=in_specs, out_sp...  70.8 us
    all_to_all x5, starting transfers between devices, swap(): return lax.all_to_all(x, axes, 0, 0, tiled=True)  30.6 us
    all_to_all x1, blocking collectives, swap(): return lax.all_to_all(x, axes, 0, 0, tiled=True)  16.5 us
    all_to_all x5, waiting for transfers between devices, swap(): return lax.all_to_all(x, axes, 0, 0, tiled=True)  7.24 us
  transfers between devices with their start and end apart: 5, of which 3 were waited for; matrix products, arithmetic and copies ran while one was open for 0% of the time, Pallas kernels for 35%

profile of v3, /device:TPU:1, one launch (start us, length us, event | category | flops | bytes accessed | tf_op | source)
XLA Modules:
  0.0 126.5 jit_solution(3510004749680067598)
XLA Ops:
  0.6 0.0 copy-start.1
  0.7 1.8 %pack.1 = (f32[8,768]{1,0:T(8,128)S(1)}, f32[2,8,640]{2,1,0:T(8,128)S(1)}, f32[16,8,768]{2,1,0:T(8,128)S(1)}, f32[16,2,8,640]{3,2,1,0:T(8,128)}) custom-call(f32[1]{0:T(128)} %bitcast.2.centre, f32[3,768]{1,0:T(4,128)} %refs_0_.4, f32[6,128]{1,0:T(8,128)} %bitcast.14, f32[3,768]{1,0:T(4,128)} %refs_2_.1, f32[3,2,544]{2,1,0:T(2,128)} %bitcast.12, ...), custom_call_target="tpu_custom_call" | custom-call | tf_op jit(solution)/shard_map/pack/pallas_call | solution.py:162
  2.4 16.5 %all_to_all.36.group = f32[16,8,768]{2,1,0:T(8,128)S(1)} all-to-all(f32[16,8,768]{2,1,0:T(8,128)S(1)} %get-tuple-element.21), channel_id=1, replica_groups=mesh['wall'=8,'cell'=16] {'cell'}, dimensions={0} | all-to-all | bytes 786432 | tf_op jit(solution)/shard_map/all_to_all | solution.py:456
  18.9 4.1 %all-to-all-start.2 = ((f32[16,2,8,640]{3,2,1,0:T(8,128)}), f32[16,2,8,640]{3,2,1,0:T(8,128)S(1)}, u32[]{:S(2)}, u32[]{:S(2)}) async-start(f32[16,2,8,640]{3,2,1,0:T(8,128)} %get-tuple-element.26), calls=%async_computation.2 | async-start | bytes 1310720 | tf_op jit(solution)/shard_map/all_to_all | solution.py:456
  23.1 14.0 %first.1 = (bf16[16,768,768]{2,1,0:T(8,128)(2,1)}, f32[16,4,768]{2,1,0:T(4,128)}, f32[1,128]{1,0:T(1,128)S(1)}) custom-call(f32[8,768]{1,0:T(8,128)S(1)} %get-tuple-element.20.mine, f32[16,8,768]{2,1,0:T(8,128)S(1)} %all_to_all.36.group), custom_call_target="tpu_custom_call" | custom-call | tf_op jit(solution)/shard_map/first/pallas_call | solution.py:162
  37.1 0.0 all-to-all-done.2.refs_2_
  37.1 6.7 %all-to-all-start.1 = ((f32[16,4,768]{2,1,0:T(4,128)}), f32[16,4,768]{2,1,0:T(4,128)S(1)}, u32[]{:S(2)}, u32[]{:S(2)}) async-start(f32[16,4,768]{2,1,0:T(4,128)} %get-tuple-element.24), calls=%async_computation.1 | async-start | bytes 393216 | tf_op jit(solution)/shard_map/all_to_all | solution.py:456
  43.7 0.0 copy-start
  43.8 0.7 copy-done
  44.4 4.3 %near0.1.after = f32[2,4,544]{2,1,0:T(4,128)S(1)} custom-call(s32[2,8]{1,0:T(2,128)S(1)} %copy-done, f32[2,8,640]{2,1,0:T(8,128)S(1)} %get-tuple-element.25.refs_1_.own, f32[16,2,8,640]{3,2,1,0:T(8,128)S(1)} %all-to-all-done.2.refs_2_), custom_call_target="tpu_custom_call" | custom-call | tf_op jit(solution)/shard_map/near0/pallas_call | solution.py:162
  48.7 2.0 %all-to-all-done.1.image = f32[16,4,768]{2,1,0:T(4,128)S(1)} async-done(((f32[16,4,768]{2,1,0:T(4,128)}), f32[16,4,768]{2,1,0:T(4,128)S(1)}, u32[]{:S(2)}, u32[]{:S(2)}) %all-to-all-start.1) | async-done | bytes 196640 | tf_op jit(solution)/shard_map/all_to_all | solution.py:456
  50.7 7.9 %second.1 = (f32[16,4,768]{2,1,0:T(4,128)S(1)}, f32[16,4,768]{2,1,0:T(4,128)}, f32[1,128]{1,0:T(1,128)S(1)}) custom-call(f32[8,768]{1,0:T(8,128)S(1)} %get-tuple-element.20.mine, f32[16,8,768]{2,1,0:T(8,128)S(1)} %all_to_all.36.group, bf16[16,768,768]{2,1,0:T(8,128)(2,1)} %get-tuple-element.22.store, f32[1,128]{1,0:T(1,128)S(1)} %get-tuple-element.23.state0, ...), custom_call_target="tpu_custom_call" | custom-call | tf_op jit(solution)/shard_map/second/pallas_call | solution.py:162
  58.6 4.7 %all-to-all-start.3 = ((f32[16,4,768]{2,1,0:T(4,128)}), f32[16,4,768]{2,1,0:T(4,128)S(1)}, u32[]{:S(2)}, u32[]{:S(2)}) async-start(f32[16,4,768]{2,1,0:T(4,128)} %get-tuple-element.29), calls=%async_computation.3 | async-start | bytes 393216 | tf_op jit(solution)/shard_map/all_to_all | solution.py:456
  63.3 0.0 copy-done.1
  63.3 4.3 %near1.1.after = f32[2,4,544]{2,1,0:T(4,128)S(1)} custom-call(s32[2,8]{1,0:T(2,128)S(1)} %copy-done.1, f32[2,8,640]{2,1,0:T(8,128)S(1)} %get-tuple-element.25.refs_1_.own, f32[16,2,8,640]{3,2,1,0:T(8,128)S(1)} %all-to-all-done.2.refs_2_), custom_call_target="tpu_custom_call" | custom-call | tf_op jit(solution)/shard_map/near1/pallas_call | solution.py:162
  67.6 2.6 %all-to-all-done.3.image = f32[16,4,768]{2,1,0:T(4,128)S(1)} async-done(((f32[16,4,768]{2,1,0:T(4,128)}), f32[16,4,768]{2,1,0:T(4,128)S(1)}, u32[]{:S(2)}, u32[]{:S(2)}) %all-to-all-start.3) | async-done | bytes 196640 | tf_op jit(solution)/shard_map/all_to_all | solution.py:456
  70.2 7.9 %third.1 = (f32[16,4,768]{2,1,0:T(4,128)S(1)}, f32[16,4,768]{2,1,0:T(4,128)}, f32[1,128]{1,0:T(1,128)S(1)}) custom-call(f32[8,768]{1,0:T(8,128)S(1)} %get-tuple-element.20.mine, f32[16,8,768]{2,1,0:T(8,128)S(1)} %all_to_all.36.group, bf16[16,768,768]{2,1,0:T(8,128)(2,1)} %get-tuple-element.22.store, f32[1,128]{1,0:T(1,128)S(1)} %get-tuple-element.23.state0, ...), custom_call_target="tpu_custom_call" | custom-call | tf_op jit(solution)/shard_map/third/pallas_call | solution.py:162
  78.1 4.1 %all-to-all-start.4 = ((f32[16,4,768]{2,1,0:T(4,128)}), f32[16,4,768]{2,1,0:T(4,128)S(1)}, u32[]{:S(2)}, u32[]{:S(2)}) async-start(f32[16,4,768]{2,1,0:T(4,128)} %get-tuple-element.32), calls=%async_computation.4 | async-start | bytes 393216 | tf_op jit(solution)/shard_map/all_to_all | solution.py:456
  82.2 4.3 %near2.1.after = f32[2,4,544]{2,1,0:T(4,128)S(1)} custom-call(s32[2,8]{1,0:T(2,128)S(1)} %copy-done.1, f32[2,8,640]{2,1,0:T(8,128)S(1)} %get-tuple-element.25.refs_1_.own, f32[16,2,8,640]{3,2,1,0:T(8,128)S(1)} %all-to-all-done.2.refs_2_), custom_call_target="tpu_custom_call" | custom-call | tf_op jit(solution)/shard_map/near2/pallas_call | solution.py:162
  86.5 2.6 %all-to-all-done.4.image = f32[16,4,768]{2,1,0:T(4,128)S(1)} async-done(((f32[16,4,768]{2,1,0:T(4,128)}), f32[16,4,768]{2,1,0:T(4,128)S(1)}, u32[]{:S(2)}, u32[]{:S(2)}) %all-to-all-start.4) | async-done | bytes 196640 | tf_op jit(solution)/shard_map/all_to_all | solution.py:456
  89.1 8.0 %fourth.1 = (f32[16,4,768]{2,1,0:T(4,128)S(1)}, f32[4,4,768]{2,1,0:T(4,128)S(1)}, f32[128,128]{1,0:T(8,128)}) custom-call(s32[1]{0:T(128)} %bitcast.1.at, f32[8,768]{1,0:T(8,128)S(1)} %get-tuple-element.20.mine, f32[16,8,768]{2,1,0:T(8,128)S(1)} %all_to_all.36.group, bf16[16,768,768]{2,1,0:T(8,128)(2,1)} %get-tuple-element.22.store, ...), custom_call_target="tpu_custom_call" | custom-call | tf_op jit(solution)/shard_map/fourth/pallas_call | solution.py:162
  97.1 11.0 %all-to-all-start.5 = ((f32[128,1,128]{2,1,0:T(1,128)}), f32[128,1,128]{2,1,0:T(1,128)S(1)}, u32[]{:S(2)}, u32[]{:S(2)}) async-start(f32[128,1,128]{2,1,0:T(1,128)} %bitcast.7), calls=%async_computation.5 | async-start | bytes 131072 | tf_op jit(solution)/shard_map/all_to_all | solution.py:456
  108.1 17.4 %cells.1.wall = f32[4,2,4,544]{3,2,1,0:T(4,128)S(1)} custom-call(f32[1]{0:T(128)} %bitcast.2.centre, f32[1,128]{1,0:T(1,128)S(1)} %get-tuple-element.23.state0, f32[2,8,640]{2,1,0:T(8,128)S(1)} %get-tuple-element.25.refs_1_.own, f32[16,8,768]{2,1,0:T(8,128)S(1)} %all_to_all.36.group, f32[16,4,768]{2,1,0:T(4,128)S(1)} %get-tuple-element.28.q1, ...), custom_call_target="tpu_custom_call" | custom-call | tf_op jit(solution)/shard_map/cells/pallas_call | solution.py:162
  125.5 0.0 all-to-all-done.5
  125.5 1.0 last.1
Async XLA Ops:
  0.6 62.7 %copy-start.1 = (s32[2,8]{1,0:T(2,128)S(1)}, s32[2,8]{1,0:T(2,128)}, u32[]{:S(2)}) copy-start(s32[2,8]{1,0:T(2,128)} %refs_0_.7) | copy-start | bytes 196
  18.9 18.1 %all-to-all-start.2 = ((f32[16,2,8,640]{3,2,1,0:T(8,128)}), f32[16,2,8,640]{3,2,1,0:T(8,128)S(1)}, u32[]{:S(2)}, u32[]{:S(2)}) async-start(f32[16,2,8,640]{3,2,1,0:T(8,128)} %get-tuple-element.26), calls=%async_computation.2 | async-start | bytes 1310720 | tf_op jit(solution)/shard_map/all_to_all | solution.py:456
  37.1 13.6 %all-to-all-start.1 = ((f32[16,4,768]{2,1,0:T(4,128)}), f32[16,4,768]{2,1,0:T(4,128)S(1)}, u32[]{:S(2)}, u32[]{:S(2)}) async-start(f32[16,4,768]{2,1,0:T(4,128)} %get-tuple-element.24), calls=%async_computation.1 | async-start | bytes 393216 | tf_op jit(solution)/shard_map/all_to_all | solution.py:456
  43.7 0.7 copy-start
  58.6 11.6 %all-to-all-start.3 = ((f32[16,4,768]{2,1,0:T(4,128)}), f32[16,4,768]{2,1,0:T(4,128)S(1)}, u32[]{:S(2)}, u32[]{:S(2)}) async-start(f32[16,4,768]{2,1,0:T(4,128)} %get-tuple-element.29), calls=%async_computation.3 | async-start | bytes 393216 | tf_op jit(solution)/shard_map/all_to_all | solution.py:456
  78.1 11.0 %all-to-all-start.4 = ((f32[16,4,768]{2,1,0:T(4,128)}), f32[16,4,768]{2,1,0:T(4,128)S(1)}, u32[]{:S(2)}, u32[]{:S(2)}) async-start(f32[16,4,768]{2,1,0:T(4,128)} %get-tuple-element.32), calls=%async_computation.4 | async-start | bytes 393216 | tf_op jit(solution)/shard_map/all_to_all | solution.py:456
  97.1 28.4 %all-to-all-start.5 = ((f32[128,1,128]{2,1,0:T(1,128)}), f32[128,1,128]{2,1,0:T(1,128)S(1)}, u32[]{:S(2)}, u32[]{:S(2)}) async-start(f32[128,1,128]{2,1,0:T(1,128)} %bitcast.7), calls=%async_computation.5 | async-start | bytes 131072 | tf_op jit(solution)/shard_map/all_to_all | solution.py:456

commit v4 on v3

--- a/solution.py
+++ b/solution.py
@@ -175,30 +175,38 @@
     return jax.ShapeDtypeStruct(dims, dtype)
 
 
-def pack_body(centre, *refs):
-    count = 6
-    given, (mine, own, sent_wall, sent_cells) = refs[:count], refs[count : count + 4]
-    held, sems = refs[count + 4 : 2 * count + 4], refs[2 * count + 4]
-    moves = [pltpu.make_async_copy(x, y, sems.at[k]) for k, (x, y) in enumerate(zip(given, held))]
-    for m in moves:
-        m.start()
-    for m in moves:
-        m.wait()
-    points, area, data, cell_points, cell_force, cell_weight = held
+def held(body, count):
+    def kernel(*refs):
+        given, rest, copies, sems = refs[:count], refs[count : -count - 1], refs[-count - 1 : -1], refs[-1]
+        moves = [pltpu.make_async_copy(x, y, sems.at[k]) for k, (x, y) in enumerate(zip(given, copies))]
+        for m in moves:
+            m.start()
+        for m in moves:
+            m.wait()
+        body(*copies, *rest)
+
+    return kernel
+
+
+def pack_wall_body(points, area, data, centre, mine, sent):
     n = points.shape[1]
     row = lax.broadcasted_iota(jnp.int32, (3, n), 0)
     mine[0:3] = points[...] - jnp.where(row == 0, centre[0], 0.0)
     mine[3:4] = jnp.concatenate([area[k : k + 1] for k in range(area.shape[0])], axis=1)
     mine[4:7] = data[...]
     mine[7:8] = jnp.zeros((1, n), F32)
+    for p in range(sent.shape[0]):
+        sent[p] = mine[...]
+
+
+def pack_cells_body(cell_points, cell_force, cell_weight, own, sent):
     used = cell_points.shape[2]
     own[...] = jnp.zeros_like(own)
     for i in range(own.shape[0]):
         own[i, 0:3, 0:used] = cell_points[:, i, :]
         own[i, 4:7, 0:used] = cell_force[:, i, :] * cell_weight[i : i + 1, :]
-    for p in range(sent_wall.shape[0]):
-        sent_wall[p] = mine[...]
-        sent_cells[p] = own[...]
+    for p in range(sent.shape[0]):
+        sent[p] = own[...]
 
 
 def near_body(first, partners, own, everyone, out, sources, acc):
@@ -268,11 +276,13 @@
         kept[c] = add_chunk(acc, upright(source_factor(pts)), targets, moments, HILO_FIRST)
         return 0
 
-    through(group.shape[0], step, after=lambda k: parcel(kept, store, sems, k, False).start())
+    count = store.shape[0]
+    through(count, step, after=lambda k: parcel(kept, store, sems, k, False).start())
+    lax.fori_loop(count, group.shape[0], step, 0)
     vel = velocity(mine[...], acc[...])
     for p in range(out.shape[0]):
         out[p] = vel
-    each(group.shape[0] // PART, lambda k: parcel(kept, store, sems, k, False).wait())
+    each(count // PART, lambda k: parcel(kept, store, sems, k, False).wait())
 
 
 def fetch(store, kept, sems):
@@ -306,8 +316,17 @@
         acc[...] += jnp.dot(now, kept[c], preferred_element_type=F32)
         return 0
 
-    ready[0] = moments(0)
-    through(chunks, step, before=lambda k: parcel(kept, store, sems, k, True).wait())
+    def again(c, _):
+        now = ready[c % 2]
+        ready[(c + 1) % 2] = moments((c + 1) % chunks)
+        add_chunk(acc, upright(source_factor(group[c])), targets, now, False)
+        return 0
+
+    count = store.shape[0]
+    targets = target_factor(mine[...]).astype(BF16)
+    ready[count % 2] = moments(count)
+    lax.fori_loop(count, chunks, again, 0)
+    through(count, step, before=lambda k: parcel(kept, store, sems, k, True).wait())
     return velocity(mine[...], acc[...])
 
 
@@ -450,6 +469,7 @@
 TINY = 1e-30
 THREE = 3
 PART = 2
+AGAIN = 2
 
 
 def swap(x, axes):
@@ -467,22 +487,31 @@
 
     copies = shape(peers, 4, points)
     row = shape(1, 128)
-    given = (
-        wall_points,
-        wall_area.reshape(points // 128, 128),
-        wall_data,
-        jnp.transpose(cell_points, (1, 0, 2)),
-        jnp.transpose(cell_force, (1, 0, 2)),
-        cell_weight,
-    )
-    mine, own, sent_wall, sent_cells = call(
-        pack_body,
-        [shape(8, points), shape(cells, 8, width), shape(peers, 8, points), shape(peers, cells, 8, width)],
-        (centre[None], *(pltpu.with_memory_space_constraint(x, pltpu.HBM) for x in given)),
-        "pack",
-        [pltpu.VMEM(x.shape, F32) for x in given] + [pltpu.SemaphoreType.DMA((len(given),))],
-        smem=(0,),
-        apart=range(1, 1 + len(given)),
+    def pack(body, outs, given, more, name):
+        given = [pltpu.with_memory_space_constraint(x, pltpu.HBM) for x in given]
+        return call(
+            held(body, 3),
+            outs,
+            (*given, *more),
+            name,
+            [pltpu.VMEM(x.shape, F32) for x in given] + [pltpu.SemaphoreType.DMA((3,))],
+            smem=(3,),
+            apart=(0, 1, 2),
+        )
+
+    mine, sent_wall = pack(
+        pack_wall_body,
+        [shape(8, points), shape(peers, 8, points)],
+        (wall_points, wall_area.reshape(points // 128, 128), wall_data),
+        (centre[None],),
+        "pack_wall",
+    )
+    own, sent_cells = pack(
+        pack_cells_body,
+        [shape(cells, 8, width), shape(peers, cells, 8, width)],
+        (jnp.transpose(cell_points, (1, 0, 2)), jnp.transpose(cell_force, (1, 0, 2)), cell_weight),
+        (),
+        "pack_cells",
     )
     group = swap(sent_wall, "cell")
     everyone = swap(sent_cells, "cell")
@@ -491,7 +520,7 @@
         pltpu.VMEM((48, points), F32),
         pltpu.SemaphoreType.DMA((peers // PART,)),
     )
-    later = (scratch[0], pltpu.VMEM((2, 48, points), BF16), *scratch[1:])
+    later = (pltpu.VMEM((peers - AGAIN, points, points), BF16), pltpu.VMEM((2, 48, points), BF16), *scratch[1:])
 
     def near(k):
         return call(
@@ -505,7 +534,7 @@
 
     store, s0, state0 = call(
         first_body,
-        [shape(peers, points, points, dtype=BF16), copies, row],
+        [shape(peers - AGAIN, points, points, dtype=BF16), copies, row],
         (mine, group),
         "first",
         scratch,

time: 127 us -> 124 us (0.976)
  blocking collectives: 16.5 us -> 0 us
  starting transfers between devices: 30.6 us -> 39 us
  waiting for transfers between devices: 7.24 us -> 13.8 us
  Pallas kernels: 70.8 us -> 68.9 us
    all_to_all x1 -> x0, blocking collectives: 16.5 us -> none  [swap(): return lax.all_to_all(x, axes, 0, 0, tiled=True)]
    all_to_all x5 -> x6, starting transfers between devices: 30.6 us -> 39 us  [swap(): return lax.all_to_all(x, axes, 0, 0, tiled=True)]
    all_to_all x5 -> x6, waiting for transfers between devices: 7.24 us -> 13.8 us  [swap(): return lax.all_to_all(x, axes, 0, 0, tiled=True)]
    pallas_call x10 -> x11, Pallas kernels: 70.8 us -> 68.9 us  [call(): pl.pallas_call(body, grid=(1,), out_shape=outs, in_specs=in_specs, out_sp...]
  transfers between devices with their start and end apart: 5 -> 6, of which waited for: 3 -> 4; matrix products, arithmetic and copies ran while one was open for 0% -> 0% of each run, Pallas kernels for 35% -> 36%
where the time goes in v4:
time: 124 us; the launch traced here: 123 us
  Pallas kernels  68.9 us (56%)
  starting transfers between devices  39 us (31%)
  waiting for transfers between devices  13.8 us (11%)
    pallas_call x11, Pallas kernels, call(): pl.pallas_call(body, grid=(1,), out_shape=outs, in_specs=in_specs, out_sp...  68.9 us
    all_to_all x6, starting transfers between devices, swap(): return lax.all_to_all(x, axes, 0, 0, tiled=True)  39 us
    all_to_all x6, waiting for transfers between devices, swap(): return lax.all_to_all(x, axes, 0, 0, tiled=True)  13.8 us
  transfers between devices with their start and end apart: 6, of which 4 were waited for; matrix products, arithmetic and copies ran while one was open for 0% of the time, Pallas kernels for 36%

profile of v4, /device:TPU:1, one launch (start us, length us, event | category | flops | bytes accessed | tf_op | source)
XLA Modules:
  0.0 123.2 jit_solution(5028114203545679966)
XLA Ops:
  0.6 0.0 copy-start.1
  0.7 1.6 %pack_wall.1 = (f32[8,768]{1,0:T(8,128)S(1)}, f32[16,8,768]{2,1,0:T(8,128)}) custom-call(f32[3,768]{1,0:T(4,128)} %refs_0_.4, f32[6,128]{1,0:T(8,128)} %bitcast.14, f32[3,768]{1,0:T(4,128)} %refs_2_.2, f32[1]{0:T(128)} %bitcast.3.refs_3_.centre), custom_call_target="tpu_custom_call" | custom-call | tf_op jit(solution)/shard_map/pack_wall/pallas_call | solution.py:162
  2.2 8.4 %all-to-all-start = ((f32[16,8,768]{2,1,0:T(8,128)}), f32[16,8,768]{2,1,0:T(8,128)S(1)}, u32[]{:S(2)}, u32[]{:S(2)}) async-start(f32[16,8,768]{2,1,0:T(8,128)} %get-tuple-element.21), calls=%async_computation | async-start | bytes 786432 | tf_op jit(solution)/shard_map/all_to_all | solution.py:476
  10.7 1.7 %pack_cells.1 = (f32[2,8,640]{2,1,0:T(8,128)S(1)}, f32[16,2,8,640]{3,2,1,0:T(8,128)}) custom-call(f32[3,2,544]{2,1,0:T(2,128)} %bitcast.12, f32[3,2,544]{2,1,0:T(2,128)} %bitcast.13, f32[2,544]{1,0:T(2,128)} %refs_2_.3), custom_call_target="tpu_custom_call" | custom-call | tf_op jit(solution)/shard_map/pack_cells/pallas_call | solution.py:162
  12.3 6.6 %all-to-all-done.group = f32[16,8,768]{2,1,0:T(8,128)S(1)} async-done(((f32[16,8,768]{2,1,0:T(8,128)}), f32[16,8,768]{2,1,0:T(8,128)S(1)}, u32[]{:S(2)}, u32[]{:S(2)}) %all-to-all-start) | async-done | bytes 393248 | tf_op jit(solution)/shard_map/all_to_all | solution.py:476
  18.9 4.1 %all-to-all-start.2 = ((f32[16,2,8,640]{3,2,1,0:T(8,128)}), f32[16,2,8,640]{3,2,1,0:T(8,128)S(1)}, u32[]{:S(2)}, u32[]{:S(2)}) async-start(f32[16,2,8,640]{3,2,1,0:T(8,128)} %get-tuple-element.26), calls=%async_computation.2 | async-start | bytes 1310720 | tf_op jit(solution)/shard_map/all_to_all | solution.py:476
  23.1 12.7 %first.1 = (bf16[14,768,768]{2,1,0:T(8,128)(2,1)}, f32[16,4,768]{2,1,0:T(4,128)}, f32[1,128]{1,0:T(1,128)S(1)}) custom-call(f32[8,768]{1,0:T(8,128)S(1)} %get-tuple-element.20.mine, f32[16,8,768]{2,1,0:T(8,128)S(1)} %all-to-all-done.group), custom_call_target="tpu_custom_call" | custom-call | tf_op jit(solution)/shard_map/first/pallas_call | solution.py:162
  35.7 0.0 all-to-all-done.2.refs_2_
  35.8 6.7 %all-to-all-start.1 = ((f32[16,4,768]{2,1,0:T(4,128)}), f32[16,4,768]{2,1,0:T(4,128)S(1)}, u32[]{:S(2)}, u32[]{:S(2)}) async-start(f32[16,4,768]{2,1,0:T(4,128)} %get-tuple-element.24), calls=%async_computation.1 | async-start | bytes 393216 | tf_op jit(solution)/shard_map/all_to_all | solution.py:476
  42.4 0.0 copy-start
  42.4 0.7 copy-done
  43.1 4.3 %near0.1.after = f32[2,4,544]{2,1,0:T(4,128)S(1)} custom-call(s32[2,8]{1,0:T(2,128)S(1)} %copy-done, f32[2,8,640]{2,1,0:T(8,128)S(1)} %get-tuple-element.25.refs_1_.own, f32[16,2,8,640]{3,2,1,0:T(8,128)S(1)} %all-to-all-done.2.refs_2_), custom_call_target="tpu_custom_call" | custom-call | tf_op jit(solution)/shard_map/near0/pallas_call | solution.py:162
  47.4 2.0 %all-to-all-done.1.image = f32[16,4,768]{2,1,0:T(4,128)S(1)} async-done(((f32[16,4,768]{2,1,0:T(4,128)}), f32[16,4,768]{2,1,0:T(4,128)S(1)}, u32[]{:S(2)}, u32[]{:S(2)}) %all-to-all-start.1) | async-done | bytes 196640 | tf_op jit(solution)/shard_map/all_to_all | solution.py:476
  49.4 7.2 %second.1 = (f32[16,4,768]{2,1,0:T(4,128)S(1)}, f32[16,4,768]{2,1,0:T(4,128)}, f32[1,128]{1,0:T(1,128)S(1)}) custom-call(f32[8,768]{1,0:T(8,128)S(1)} %get-tuple-element.20.mine, f32[16,8,768]{2,1,0:T(8,128)S(1)} %all-to-all-done.group, bf16[14,768,768]{2,1,0:T(8,128)(2,1)} %get-tuple-element.22.store, f32[1,128]{1,0:T(1,128)S(1)} %get-tuple-element.23.state0, ...), custom_call_target="tpu_custom_call" | custom-call | tf_op jit(solution)/shard_map/second/pallas_call | solution.py:162
  56.6 4.7 %all-to-all-start.3 = ((f32[16,4,768]{2,1,0:T(4,128)}), f32[16,4,768]{2,1,0:T(4,128)S(1)}, u32[]{:S(2)}, u32[]{:S(2)}) async-start(f32[16,4,768]{2,1,0:T(4,128)} %get-tuple-element.29), calls=%async_computation.3 | async-start | bytes 393216 | tf_op jit(solution)/shard_map/all_to_all | solution.py:476
  61.3 0.0 copy-done.1
  61.3 4.3 %near1.1.after = f32[2,4,544]{2,1,0:T(4,128)S(1)} custom-call(s32[2,8]{1,0:T(2,128)S(1)} %copy-done.1, f32[2,8,640]{2,1,0:T(8,128)S(1)} %get-tuple-element.25.refs_1_.own, f32[16,2,8,640]{3,2,1,0:T(8,128)S(1)} %all-to-all-done.2.refs_2_), custom_call_target="tpu_custom_call" | custom-call | tf_op jit(solution)/shard_map/near1/pallas_call | solution.py:162
  65.6 2.6 %all-to-all-done.3.image = f32[16,4,768]{2,1,0:T(4,128)S(1)} async-done(((f32[16,4,768]{2,1,0:T(4,128)}), f32[16,4,768]{2,1,0:T(4,128)S(1)}, u32[]{:S(2)}, u32[]{:S(2)}) %all-to-all-start.3) | async-done | bytes 196640 | tf_op jit(solution)/shard_map/all_to_all | solution.py:476
  68.2 7.2 %third.1 = (f32[16,4,768]{2,1,0:T(4,128)S(1)}, f32[16,4,768]{2,1,0:T(4,128)}, f32[1,128]{1,0:T(1,128)S(1)}) custom-call(f32[8,768]{1,0:T(8,128)S(1)} %get-tuple-element.20.mine, f32[16,8,768]{2,1,0:T(8,128)S(1)} %all-to-all-done.group, bf16[14,768,768]{2,1,0:T(8,128)(2,1)} %get-tuple-element.22.store, f32[1,128]{1,0:T(1,128)S(1)} %get-tuple-element.23.state0, ...), custom_call_target="tpu_custom_call" | custom-call | tf_op jit(solution)/shard_map/third/pallas_call | solution.py:162
  75.5 4.1 %all-to-all-start.4 = ((f32[16,4,768]{2,1,0:T(4,128)}), f32[16,4,768]{2,1,0:T(4,128)S(1)}, u32[]{:S(2)}, u32[]{:S(2)}) async-start(f32[16,4,768]{2,1,0:T(4,128)} %get-tuple-element.32), calls=%async_computation.4 | async-start | bytes 393216 | tf_op jit(solution)/shard_map/all_to_all | solution.py:476
  79.6 4.3 %near2.1.after = f32[2,4,544]{2,1,0:T(4,128)S(1)} custom-call(s32[2,8]{1,0:T(2,128)S(1)} %copy-done.1, f32[2,8,640]{2,1,0:T(8,128)S(1)} %get-tuple-element.25.refs_1_.own, f32[16,2,8,640]{3,2,1,0:T(8,128)S(1)} %all-to-all-done.2.refs_2_), custom_call_target="tpu_custom_call" | custom-call | tf_op jit(solution)/shard_map/near2/pallas_call | solution.py:162
  83.8 2.6 %all-to-all-done.4.image = f32[16,4,768]{2,1,0:T(4,128)S(1)} async-done(((f32[16,4,768]{2,1,0:T(4,128)}), f32[16,4,768]{2,1,0:T(4,128)S(1)}, u32[]{:S(2)}, u32[]{:S(2)}) %all-to-all-start.4) | async-done | bytes 196640 | tf_op jit(solution)/shard_map/all_to_all | solution.py:476
  86.5 7.3 %fourth.1 = (f32[16,4,768]{2,1,0:T(4,128)S(1)}, f32[4,4,768]{2,1,0:T(4,128)S(1)}, f32[128,128]{1,0:T(8,128)}) custom-call(s32[1]{0:T(128)} %bitcast.1.at, f32[8,768]{1,0:T(8,128)S(1)} %get-tuple-element.20.mine, f32[16,8,768]{2,1,0:T(8,128)S(1)} %all-to-all-done.group, bf16[14,768,768]{2,1,0:T(8,128)(2,1)} %get-tuple-element.22.store, ...), custom_call_target="tpu_custom_call" | custom-call | tf_op jit(solution)/shard_map/fourth/pallas_call | solution.py:162
  93.8 11.0 %all-to-all-start.5 = ((f32[128,1,128]{2,1,0:T(1,128)}), f32[128,1,128]{2,1,0:T(1,128)S(1)}, u32[]{:S(2)}, u32[]{:S(2)}) async-start(f32[128,1,128]{2,1,0:T(1,128)} %bitcast.7), calls=%async_computation.5 | async-start | bytes 131072 | tf_op jit(solution)/shard_map/all_to_all | solution.py:476
  104.8 17.4 %cells.1.wall = f32[4,2,4,544]{3,2,1,0:T(4,128)S(1)} custom-call(f32[1]{0:T(128)} %bitcast.3.refs_3_.centre, f32[1,128]{1,0:T(1,128)S(1)} %get-tuple-element.23.state0, f32[2,8,640]{2,1,0:T(8,128)S(1)} %get-tuple-element.25.refs_1_.own, f32[16,8,768]{2,1,0:T(8,128)S(1)} %all-to-all-done.group, f32[16,4,768]{2,1,0:T(4,128)S(1)} %get-tuple-element.28.q1, ...), custom_call_target="tpu_custom_call" | custom-call | tf_op jit(solution)/shard_map/cells/pallas_call | solution.py:162
  122.2 0.0 all-to-all-done.5
  122.2 1.0 last.1
Async XLA Ops:
  0.6 60.7 %copy-start.1 = (s32[2,8]{1,0:T(2,128)S(1)}, s32[2,8]{1,0:T(2,128)}, u32[]{:S(2)}) copy-start(s32[2,8]{1,0:T(2,128)} %refs_0_.7) | copy-start | bytes 196
  2.2 16.7 %all-to-all-start = ((f32[16,8,768]{2,1,0:T(8,128)}), f32[16,8,768]{2,1,0:T(8,128)S(1)}, u32[]{:S(2)}, u32[]{:S(2)}) async-start(f32[16,8,768]{2,1,0:T(8,128)} %get-tuple-element.21), calls=%async_computation | async-start | bytes 786432 | tf_op jit(solution)/shard_map/all_to_all | solution.py:476
  18.9 16.8 %all-to-all-start.2 = ((f32[16,2,8,640]{3,2,1,0:T(8,128)}), f32[16,2,8,640]{3,2,1,0:T(8,128)S(1)}, u32[]{:S(2)}, u32[]{:S(2)}) async-start(f32[16,2,8,640]{3,2,1,0:T(8,128)} %get-tuple-element.26), calls=%async_computation.2 | async-start | bytes 1310720 | tf_op jit(solution)/shard_map/all_to_all | solution.py:476
  35.8 13.6 %all-to-all-start.1 = ((f32[16,4,768]{2,1,0:T(4,128)}), f32[16,4,768]{2,1,0:T(4,128)S(1)}, u32[]{:S(2)}, u32[]{:S(2)}) async-start(f32[16,4,768]{2,1,0:T(4,128)} %get-tuple-element.24), calls=%async_computation.1 | async-start | bytes 393216 | tf_op jit(solution)/shard_map/all_to_all | solution.py:476
  42.4 0.7 copy-start
  56.6 11.6 %all-to-all-start.3 = ((f32[16,4,768]{2,1,0:T(4,128)}), f32[16,4,768]{2,1,0:T(4,128)S(1)}, u32[]{:S(2)}, u32[]{:S(2)}) async-start(f32[16,4,768]{2,1,0:T(4,128)} %get-tuple-element.29), calls=%async_computation.3 | async-start | bytes 393216 | tf_op jit(solution)/shard_map/all_to_all | solution.py:476
  75.5 11.0 %all-to-all-start.4 = ((f32[16,4,768]{2,1,0:T(4,128)}), f32[16,4,768]{2,1,0:T(4,128)S(1)}, u32[]{:S(2)}, u32[]{:S(2)}) async-start(f32[16,4,768]{2,1,0:T(4,128)} %get-tuple-element.32), calls=%async_computation.4 | async-start | bytes 393216 | tf_op jit(solution)/shard_map/all_to_all | solution.py:476
  93.8 28.4 %all-to-all-start.5 = ((f32[128,1,128]{2,1,0:T(1,128)}), f32[128,1,128]{2,1,0:T(1,128)S(1)}, u32[]{:S(2)}, u32[]{:S(2)}) async-start(f32[128,1,128]{2,1,0:T(1,128)} %bitcast.7), calls=%async_computation.5 | async-start | bytes 131072 | tf_op jit(solution)/shard_map/all_to_all | solution.py:476
